TPU v7x, 32 devices: a whole 2x2x4 slice. The times are simulated.
32 devices in a mesh: wide: 8 (over z, x), narrow: 4 (over y, core).
Axes of the slice: x: 2, y: 2, z: 4, core: 2. Of those that a mesh axis runs over, the one named last changes fastest.
Arguments:
- tokens: bfloat16 [16384, 768], P(('wide', 'narrow')), may hold values from -6 to 6
- timestep: int32 [16], P('wide'), may hold values from 0 to 999
- token_mask: int32 [16384], P(('wide', 'narrow')), may hold values 0 or 1
- time_table: float32 [1000, 128], replicated, may hold values from -6 to 6
- w_ada: bfloat16 [128, 4608], replicated, may hold values from -0.5 to 0.5
- b_ada: float32 [4608], replicated, may hold values from -3 to 3
- gain_one: float32 [768], replicated, may hold values from 0.5 to 1.5
- w_qkv: bfloat16 [3, 768, 768], P(None, None, 'narrow'), may hold values from -0.21875 to 0.21875
- w_out: bfloat16 [768, 768], P('narrow'), may hold values from -3.5 to 3.5
- gain_two: float32 [768], replicated, may hold values from 0.5 to 1.5
- w_up: bfloat16 [768, 3072], P(None, 'narrow'), may hold values from -0.21875 to 0.21875
- b_up: float32 [3072], P('narrow'), may hold values from -3 to 3
- w_down: bfloat16 [3072, 768], P('narrow'), may hold values from -0.109375 to 0.109375
- b_down: float32 [768], replicated, may hold values from -3 to 3
- cotangent: bfloat16 [16384, 768], P(('wide', 'narrow')), may hold values from -6 to 6
Outputs:
- mixed: bfloat16 [16384, 768], P(('wide', 'narrow'))
- grad_tokens: float32 [16384, 768], P(('wide', 'narrow'))
- grad_time_table: float32 [1000, 128], replicated
- grad_w_ada: float32 [128, 4608], replicated
- grad_b_ada: float32 [4608], replicated
- grad_gain_one: float32 [768], replicated
- grad_w_qkv: float32 [3, 768, 768], P(None, None, 'narrow')
- grad_w_out: float32 [768, 768], P('narrow')
- grad_gain_two: float32 [768], replicated
- grad_w_up: float32 [768, 3072], P(None, 'narrow')
- grad_b_up: float32 [3072], P('narrow')
- grad_w_down: float32 [3072, 768], P('narrow')
- grad_b_down: float32 [768], replicated
Inputs may be any that keep to these rules, and one draw needn't show every extreme that they name: One timestep for each sequence of 1024 tokens.
All inputs are finite; a program needn't handle non-finite values. No bound on the sum of `token_mask` on one device may be relied on, other than what follows from the above.
Results may differ from a plain program's by a relative error of at most 0.02.
The roundings to bfloat16 on the way count: a program that leaves them out, or rounds other values in their place, can miss the bound.
Values may be sent and summed in bfloat16 or wider, within the bound.
A program may use at most 192 MiB of HBM per device.

v0:
```python
from functools import partial
import math

import jax
import jax.numpy as jnp
from jax import lax
from jax.sharding import PartitionSpec as P

D = 768
HD = 64
LEN = 1024
SEQS = 2


norm_eps = 1e-06
highest = lax.Precision.HIGHEST


def layer_norm(values, norm_gain):
    centered = values - jnp.mean(values, axis=-1, keepdims=True)
    variance = jnp.mean(centered * centered, axis=-1, keepdims=True)
    return centered * lax.rsqrt(variance + norm_eps) * norm_gain


def norm_back(values, norm_gain, grad_norm):
    _, pullback = jax.vjp(layer_norm, values, norm_gain)
    return pullback(grad_norm)


def rope_tables():
    half_width = HD // 2
    frequency = 10000.0 ** (-2.0 * jnp.arange(half_width, dtype=jnp.float32) / HD)
    angles = jnp.arange(LEN, dtype=jnp.float32)[:, None] * frequency[None, :]
    cos_table = jnp.concatenate([jnp.cos(angles), jnp.cos(angles)], axis=1)[:, None, :]
    sin_table = jnp.concatenate([jnp.sin(angles), jnp.sin(angles)], axis=1)[:, None, :]
    return (cos_table, sin_table)


def rotate(values, cos_table, sin_table):
    half_width = values.shape[-1] // 2
    turned = jnp.concatenate([-values[..., half_width:], values[..., :half_width]], axis=-1)
    return values * cos_table + turned * sin_table


def attend(q_low, k_low, v_low):
    scale_factor = 1.0 / math.sqrt(HD)
    block_rows = min(512, LEN)

    def one_sequence(pieces):
        q_seq, k_seq, v_seq = pieces
        outputs = []
        log_parts = []
        for first_row in range(0, LEN, block_rows):
            scores = (
                jnp.einsum(
                    "qhe,khe->hqk",
                    q_seq[first_row : first_row + block_rows],
                    k_seq,
                    preferred_element_type=jnp.float32,
                )
                * scale_factor
            )
            row_max = jnp.max(scores, axis=-1, keepdims=True)
            exp_scores = jnp.exp(scores - row_max)
            row_sum = jnp.sum(exp_scores, axis=-1, keepdims=True)
            probs_low = (exp_scores / row_sum).astype(jnp.bfloat16)
            outputs.append(
                jnp.einsum("hqk,khe->qhe", probs_low, v_seq, preferred_element_type=jnp.float32)
            )
            log_parts.append((row_max + jnp.log(row_sum))[..., 0])
        return (jnp.concatenate(outputs, axis=0), jnp.concatenate(log_parts, axis=1))

    return lax.map(one_sequence, (q_low, k_low, v_low))


def attend_back(q_low, k_low, v_low, log_sums, grad_heads):
    scale_factor = 1.0 / math.sqrt(HD)
    block_rows = min(512, LEN)

    def one_sequence(pieces):
        q_seq, k_seq, v_seq, sums_seq, grad_seq = pieces
        grad_keys = jnp.zeros(k_seq.shape, jnp.float32)
        grad_values = jnp.zeros(v_seq.shape, jnp.float32)
        grad_queries = []
        for first_row in range(0, LEN, block_rows):
            q_block = q_seq[first_row : first_row + block_rows]
            grad_block = grad_seq[first_row : first_row + block_rows]
            scores = (
                jnp.einsum("qhe,khe->hqk", q_block, k_seq, preferred_element_type=jnp.float32)
                * scale_factor
            )
            probs = jnp.exp(scores - sums_seq[:, first_row : first_row + block_rows, None])
            probs_low = probs.astype(jnp.bfloat16)
            grad_values = grad_values + jnp.einsum(
                "hqk,qhe->khe", probs_low, grad_block, preferred_element_type=jnp.float32
            )
            grad_probs = jnp.einsum(
                "qhe,khe->hqk", grad_block, v_seq, preferred_element_type=jnp.float32
            )
            inner_sum = jnp.sum(probs * grad_probs, axis=-1, keepdims=True)
            grad_scores = (probs * (grad_probs - inner_sum) * scale_factor).astype(jnp.bfloat16)
            grad_queries.append(
                jnp.einsum("hqk,khe->qhe", grad_scores, k_seq, preferred_element_type=jnp.float32)
            )
            grad_keys = grad_keys + jnp.einsum(
                "hqk,qhe->khe", grad_scores, q_block, preferred_element_type=jnp.float32
            )
        return (jnp.concatenate(grad_queries, axis=0), grad_keys, grad_values)

    return lax.map(one_sequence, (q_low, k_low, v_low, log_sums, grad_heads))


def forward(
    tokens,
    timestep,
    time_table,
    w_ada,
    b_ada,
    gain_one,
    w_qkv,
    w_out,
    gain_two,
    w_up,
    b_up,
    w_down,
    b_down,
):
    tok_rows = tokens.shape[0]
    group_heads = w_qkv.shape[2] // HD
    step_pick = (
        timestep[:, None] == jnp.arange(time_table.shape[0], dtype=jnp.int32)[None, :]
    ).astype(jnp.float32)
    picked = jnp.dot(step_pick, time_table, precision=highest)
    cond_low = jax.nn.silu(picked).astype(jnp.bfloat16)
    modulation = jnp.dot(cond_low, w_ada, preferred_element_type=jnp.float32) + b_ada
    positions = lax.axis_index("narrow") * tok_rows + jnp.arange(tok_rows, dtype=jnp.int32)
    row_pick = (positions[:, None] // LEN == jnp.arange(SEQS, dtype=jnp.int32)[None, :]).astype(
        jnp.float32
    )
    mod_tok = jnp.dot(row_pick, modulation, precision=highest).reshape(tok_rows, 6, D)
    residual_in = tokens.astype(jnp.float32)
    norm_one = layer_norm(residual_in, gain_one)
    normed_low = (norm_one * (1.0 + mod_tok[:, 1]) + mod_tok[:, 0]).astype(jnp.bfloat16)
    normed_all = lax.all_gather(normed_low, "narrow", axis=0, tiled=True)
    projected = jnp.einsum("td,kde->kte", normed_all, w_qkv, preferred_element_type=jnp.float32)
    shaped = projected.reshape(3, SEQS, LEN, group_heads, HD)
    cos_table, sin_table = rope_tables()
    q_low = rotate(shaped[0], cos_table, sin_table).astype(jnp.bfloat16)
    k_low = rotate(shaped[1], cos_table, sin_table).astype(jnp.bfloat16)
    v_low = shaped[2].astype(jnp.bfloat16)
    head_out, log_sums = attend(q_low, k_low, v_low)
    heads_low = head_out.astype(jnp.bfloat16).reshape(SEQS * LEN, group_heads * HD)
    attn_part = lax.psum_scatter(
        jnp.dot(
            lax.slice_in_dim(heads_low, 0, tok_rows * lax.axis_size("narrow"), axis=0),
            w_out,
            preferred_element_type=jnp.float32,
        ).astype(jnp.bfloat16),
        "narrow",
        scatter_dimension=0,
        tiled=True,
    ).astype(jnp.float32)
    mid_residual = residual_in + mod_tok[:, 2] * attn_part
    norm_two = layer_norm(mid_residual, gain_two)
    normed_two_low = (norm_two * (1.0 + mod_tok[:, 4]) + mod_tok[:, 3]).astype(jnp.bfloat16)
    normed_two_all = lax.all_gather(normed_two_low, "narrow", axis=0, tiled=True)
    pre_act = jnp.dot(normed_two_all, w_up, preferred_element_type=jnp.float32) + b_up
    act_low = jax.nn.gelu(pre_act, approximate=True).astype(jnp.bfloat16)
    branch = (
        lax.psum_scatter(
            jnp.dot(
                lax.slice_in_dim(act_low, 0, tok_rows * lax.axis_size("narrow"), axis=0),
                w_down,
                preferred_element_type=jnp.float32,
            ).astype(jnp.bfloat16),
            "narrow",
            scatter_dimension=0,
            tiled=True,
        ).astype(jnp.float32)
        + b_down
    )
    mixed = mid_residual + mod_tok[:, 5] * branch
    return (
        mixed,
        step_pick,
        picked,
        cond_low,
        row_pick,
        mod_tok,
        residual_in,
        norm_one,
        normed_all,
        q_low,
        k_low,
        v_low,
        log_sums,
        heads_low,
        attn_part,
        mid_residual,
        norm_two,
        normed_two_all,
        pre_act,
        act_low,
        branch,
    )


def body(
    tokens,
    timestep,
    token_mask,
    time_table,
    w_ada,
    b_ada,
    gain_one,
    w_qkv,
    w_out,
    gain_two,
    w_up,
    b_up,
    w_down,
    b_down,
    cotangent,
):
    weights = (
        time_table,
        w_ada,
        b_ada,
        gain_one,
        w_qkv,
        w_out,
        gain_two,
        w_up,
        b_up,
        w_down,
        b_down,
    )
    first_pass = forward(tokens, timestep, *weights)
    again_inputs = lax.optimization_barrier((tokens,) + weights)
    saved = forward(again_inputs[0], timestep, *again_inputs[1:])
    (
        unused_mixed,
        step_pick,
        picked,
        cond_low,
        row_pick,
        mod_tok,
        residual_in,
        norm_one,
        normed_all,
        q_low,
        k_low,
        v_low,
        log_sums,
        heads_low,
        attn_part,
        mid_residual,
        norm_two,
        normed_two_all,
        pre_act,
        act_low,
        branch,
    ) = saved
    tok_rows = tokens.shape[0]
    group_heads = w_qkv.shape[2] // HD
    grad_mixed = cotangent.astype(jnp.float32) * token_mask.astype(jnp.float32)[:, None]
    grad_gate_two = grad_mixed * branch
    grad_branch = grad_mixed * mod_tok[:, 5]
    b_down_part = jnp.sum(grad_branch, axis=0)
    branch_all = lax.all_gather(grad_branch.astype(jnp.bfloat16), "narrow", axis=0, tiled=True)
    grad_w_down = jnp.einsum("tf,td->fd", act_low, branch_all, preferred_element_type=jnp.float32)
    grad_act = jnp.einsum("td,fd->tf", branch_all, w_down, preferred_element_type=jnp.float32)
    _, gelu_pull = jax.vjp(partial(jax.nn.gelu, approximate=True), pre_act)
    grad_pre_low = gelu_pull(grad_act)[0].astype(jnp.bfloat16)
    grad_b_up = jnp.sum(grad_pre_low, axis=0, dtype=jnp.float32)
    grad_w_up = jnp.einsum(
        "td,tf->df", normed_two_all, grad_pre_low, preferred_element_type=jnp.float32
    )
    grad_normed_two = lax.psum_scatter(
        jnp.einsum(
            "tf,df->td",
            lax.slice_in_dim(grad_pre_low, 0, tok_rows * lax.axis_size("narrow"), axis=0),
            w_up,
            preferred_element_type=jnp.float32,
        ).astype(jnp.bfloat16),
        "narrow",
        scatter_dimension=0,
        tiled=True,
    ).astype(jnp.float32)
    grad_res_two, gain_two_part = norm_back(
        mid_residual, gain_two, grad_normed_two * (1.0 + mod_tok[:, 4])
    )
    grad_mid = grad_mixed + grad_res_two
    grad_gate_one = grad_mid * attn_part
    attention_all = lax.all_gather(
        (grad_mid * mod_tok[:, 2]).astype(jnp.bfloat16), "narrow", axis=0, tiled=True
    )
    grad_w_out = jnp.einsum(
        "te,td->ed", heads_low, attention_all, preferred_element_type=jnp.float32
    )
    grad_heads = jnp.einsum("td,ed->te", attention_all, w_out, preferred_element_type=jnp.float32)
    grad_heads = grad_heads.astype(jnp.bfloat16).reshape(SEQS, LEN, group_heads, HD)
    grad_queries, grad_keys, grad_values = attend_back(q_low, k_low, v_low, log_sums, grad_heads)
    cos_table, sin_table = rope_tables()
    _, rope_pull = jax.vjp(lambda values: rotate(values, cos_table, sin_table), grad_queries)
    grad_projected = jnp.stack([rope_pull(grad_queries)[0], rope_pull(grad_keys)[0], grad_values])
    grad_projected = grad_projected.reshape(3, SEQS * LEN, group_heads * HD).astype(jnp.bfloat16)
    grad_w_qkv = jnp.einsum(
        "td,kte->kde", normed_all, grad_projected, preferred_element_type=jnp.float32
    )
    grad_normed = lax.psum_scatter(
        jnp.einsum("kte,kde->td", grad_projected, w_qkv, preferred_element_type=jnp.float32).astype(
            jnp.bfloat16
        ),
        "narrow",
        scatter_dimension=0,
        tiled=True,
    ).astype(jnp.float32)
    grad_res_one, gain_one_part = norm_back(
        residual_in, gain_one, grad_normed * (1.0 + mod_tok[:, 1])
    )
    grad_tokens = grad_mid + grad_res_one
    grad_mod_flat = jnp.stack(
        [
            grad_normed,
            grad_normed * norm_one,
            grad_gate_one,
            grad_normed_two,
            grad_normed_two * norm_two,
            grad_gate_two,
        ],
        axis=1,
    ).reshape(tok_rows, 6 * D)
    mod_part = jnp.einsum("ts,tm->sm", row_pick, grad_mod_flat, precision=highest)
    grad_modulation, grad_gain_one, grad_gain_two, grad_b_down = (
        lax.psum(mod_part.astype(jnp.bfloat16), "narrow").astype(jnp.float32),
        lax.psum(gain_one_part.astype(jnp.bfloat16), "narrow").astype(jnp.float32),
        lax.psum(gain_two_part.astype(jnp.bfloat16), "narrow").astype(jnp.float32),
        lax.psum(b_down_part.astype(jnp.bfloat16), "narrow").astype(jnp.float32),
    )
    grad_b_ada = jnp.sum(grad_modulation, axis=0)
    modulation_low = grad_modulation.astype(jnp.bfloat16)
    grad_w_ada = jnp.einsum(
        "sc,sm->cm", cond_low, modulation_low, preferred_element_type=jnp.float32
    )
    grad_condition = jnp.einsum(
        "sm,cm->sc", modulation_low, w_ada, preferred_element_type=jnp.float32
    )
    _, silu_pull = jax.vjp(jax.nn.silu, picked)
    grad_time_table = jnp.einsum(
        "sn,sc->nc", step_pick, silu_pull(grad_condition)[0], precision=highest
    )
    (
        grad_time_table,
        grad_w_ada,
        grad_b_ada,
        grad_gain_one,
        grad_w_qkv,
        grad_w_out,
        grad_gain_two,
        grad_w_up,
        grad_b_up,
        grad_w_down,
        grad_b_down,
    ) = lax.psum(
        (
            grad_time_table,
            grad_w_ada,
            grad_b_ada,
            grad_gain_one,
            grad_w_qkv,
            grad_w_out,
            grad_gain_two,
            grad_w_up,
            grad_b_up,
            grad_w_down,
            grad_b_down,
        ),
        "wide",
    )
    return (
        first_pass[0].astype(jnp.bfloat16),
        grad_tokens,
        grad_time_table,
        grad_w_ada,
        grad_b_ada,
        grad_gain_one,
        grad_w_qkv,
        grad_w_out,
        grad_gain_two,
        grad_w_up,
        grad_b_up,
        grad_w_down,
        grad_b_down,
    )


def solution(mesh):
    return jax.shard_map(
        body,
        mesh=mesh,
        in_specs=(
            P(("wide", "narrow"), None),
            P("wide"),
            P(("wide", "narrow")),
            P(),
            P(),
            P(),
            P(),
            P(None, None, "narrow"),
            P("narrow", None),
            P(),
            P(None, "narrow"),
            P("narrow"),
            P("narrow", None),
            P(),
            P(("wide", "narrow"), None),
        ),
        out_specs=(
            P(("wide", "narrow"), None),
            P(("wide", "narrow"), None),
            P(),
            P(),
            P(),
            P(),
            P(None, None, "narrow"),
            P("narrow", None),
            P(),
            P(None, "narrow"),
            P("narrow"),
            P("narrow", None),
            P(),
        ),
        check_vma=False,
    )
```

profile of v0, /device:TPU:0, one launch (start us, length us, event | category | flops | bytes accessed | tf_op | source)
XLA Modules:
  0.0 1007.5 jit_solution(1180134621242601824)
XLA Ops:
  52.7 7.8 all-gather.13.cloned.1.call-done
  80.4 10.2 %all-gather.7.cloned.1.call-done = bf16[2048,768]{1,0:T(8,128)(2,1)} async-done(((bf16[512,768]{1,0:T(8,128)(2,1)}), bf16[2048,768]{1,0:T(8,128)(2,1)}) %all-gather.7.cloned.1.call-update) | async-done | bytes 3145744 | tf_op jit(solution)/shard_map/all_gather | solution.py:144
  115.5 20.3 %while.40 = (s32[]{:T(128)}, bf16[2,1024,3,64]{1,3,2,0:T(8,128)(2,1)}, f32[2,3,1024]{2,1,0:T(4,128)}, bf16[2,1024,3,64]{1,3,2,0:T(8,128)(2,1)}, bf16[2,1024,3,64...) while((s32[]{:T(128)}, bf16[2,1024,3,64]{1,3,2,0:T(8,128)(2,1)}, ...), condition=%wide.region_19.20_spmd.clone, body=%wide.region_14.19_spmd.sunk.clone | while | flops 834404352 | bytes 50670324 | solution.py:73
  151.1 29.0 %reduce-scatter.11.cloned.1.call-done = bf16[512,768]{1,0:T(8,128)(2,1)} async-done(((bf16[2048,768]{1,0:T(8,128)(2,1)}), bf16[512,768]{1,0:T(8,128)(2,1)}) %reduce-scatter.11.cloned.1.call-update) | async-done | bytes 786448 | tf_op jit(solution)/shard_map/reduce_scatter | solution.py:153
  200.0 42.5 %while.39 = (s32[]{:T(128)}, bf16[2,1024,3,64]{1,3,2,0:T(8,128)(2,1)S(1)}, bf16[2,1024,3,64]{1,3,2,0:T(8,128)(2,1)}, bf16[2,1024,3,64]{1,3,2,0:T(8,128)(2,1)}, bf16[2,1024,3,64]{1,3,2,0:T(8,128)(2,1)}) while((s32[]{:T(128)}, bf16[2,1024,3,64]{1,3,2,0:T(8,128)(2,1)S(1)}, bf16[2,1024,3,64]{1,3,2,0:T(8,128)(2,1)}, ...), condition=%wide.region_7.8_spmd.clone, body=%wide.region_2.7_spmd.sunk.clone | while | flops 821823488 | bytes 29129336 | solution.py:73
  200.1 6.2 fusion.443
  210.9 6.2 fusion.445
  221.2 6.3 fusion.443
  232.2 6.2 fusion.445
  246.8 7.5 fusion.312
  254.4 12.9 %convert_reduce_fusion = (f32[768]{0:T(1024)}, bf16[2048,768]{1,0:T(8,128)(2,1)S(1)}, bf16[2048,768]{1,0:T(8,128)(2,1)}) fusion(f32[2048,768]{1,0:T(8,128)} %fusion.312, f32[768]{0:T(1024)S(1)} %copy-done.101, bf16[2048,768]{1,0:T(8,128)(2,1)} %all-gather.11.cloned.1.call-done, bf16[768,768]{1,0:T(8,128)(2,1)S(1)} %copy-done), kind=kOutput, calls=%fused_computation.180 | convolution fusion | flops 2455239936 | bytes 16914432 | tf_op jit(solution)/shard_map/td,fd->tf/dot_general | solution.py:272
  288.5 36.5 %reduce-scatter.13.cloned.1.call-done = bf16[512,768]{1,0:T(8,128)(2,1)} async-done(((bf16[2048,768]{1,0:T(8,128)(2,1)}), bf16[512,768]{1,0:T(8,128)(2,1)}) %reduce-scatter.13.cloned.1.call-update) | async-done | bytes 786448 | tf_op jit(solution)/shard_map/reduce_scatter | solution.py:279
  335.7 27.9 %all-gather.17.cloned.1.call-done = bf16[2048,768]{1,0:T(8,128)(2,1)} async-done(((bf16[512,768]{1,0:T(8,128)(2,1)}), bf16[2048,768]{1,0:T(8,128)(2,1)}) %all-gather.17.cloned.1.call-update) | async-done | bytes 3145744 | tf_op jit(solution)/shard_map/all_gather | solution.py:295
  373.2 149.6 %while.41 = (s32[]{:T(128)}, f32[2,1024,3,64]{1,3,2,0:T(8,128)}, f32[2,1024,3,64]{1,3,2,0:T(8,128)}, bf16[2,1024,3,64]{1,3,2,0:T(8,128)(2,1)}, bf16[2,1024,3,64]...) while((s32[]{:T(128)}, f32[2,1024,3,64]{1,3,2,0:T(8,128)}, ...), condition=%wide.region_29.30_spmd.clone, body=%wide.region_26.29_spmd.sunk.clone | while | flops 2079926272 | bytes 209329936 | solution.py:110
  386.3 13.3 %fusion.471 = f32[512,3,64]{0,2,1:T(8,128)} fusion(f32[3,512,1024]{2,1,0:T(8,128)} %fusion.468, f32[3,512,1024]{2,1,0:T(8,128)} %copy-done.1, f32[3,512]{1,0:T(4,128)S(1)} %get-tuple-element.521, bf16[2,1024,3,64]{1,3,2,0:T(8,128)(2,1)S(1)} %get-tuple-element.590, s32[]{:T(128)S(6)} %copy.134), kind=kOutput, calls=%fused_computation.116.clone.1.clone | convolution fusion | flops 215484928 | bytes 25968644 | tf_op jit(solution)/shard_map/while/body/eval_jaxpr/hqk,khe->qhe/dot_general | solution.py:103
  404.2 13.2 %fusion.474 = f32[512,3,64]{0,2,1:T(8,128)} fusion(f32[3,512,1024]{2,1,0:T(8,128)} %fusion.472, f32[3,512,1024]{2,1,0:T(8,128)} %copy-done.2, f32[3,512]{1,0:T(4,128)S(1)} %get-tuple-element.522, bf16[2,1024,3,64]{1,3,2,0:T(8,128)(2,1)S(1)} %get-tuple-element.590, s32[]{:T(128)S(6)} %copy.134), kind=kOutput, calls=%fused_computation.117.clone.1.clone | convolution fusion | flops 215484928 | bytes 25968644 | tf_op jit(solution)/shard_map/while/body/eval_jaxpr/hqk,khe->qhe/dot_general | solution.py:103
  417.4 14.1 %fusion.476 = f32[3,64,1024]{2,1,0:T(8,128)} fusion(f32[3,512,1024]{2,1,0:T(8,128)} %fusion.472, f32[3,512,1024]{2,1,0:T(8,128)} %copy-done.2, f32[3,512]{1,0:T(4,128)S(1)} %get-tuple-element.522, bf16[2,1024,3,64]{1,3,2,0:T(8,128)(2,1)S(1)} %get-tuple-element.591, s32[]{:T(128)S(6)} %copy.134), kind=kOutput, calls=%fused_computation.91.clone.1.clone | convolution fusion | flops 215484928 | bytes 26165252 | tf_op jit(solution)/shard_map/while/body/eval_jaxpr/hqk,qhe->khe/dot_general | solution.py:105
  431.5 14.3 %fusion.477 = f32[2,1024,3,64]{1,3,2,0:T(8,128)} fusion(f32[2,1024,3,64]{1,3,2,0:T(8,128)} %get-tuple-element.579, s32[]{:T(128)S(6)} %copy.134, f32[3,64,1024]{2,1,0:T(8,128)} %fusion.476, f32[3,512,1024]{2,1,0:T(8,128)} %fusion.468, f32[3,512,1024]{2,1,0:T(8,128)} %copy-done.1, f32[3,512]{1,0:T(4,128)S(1)} %get-tuple-element.521, ...), kind=kOutput, calls=%fused_computation.115.clone.1.clone | convolution fusion | flops 215681536 | bytes 26953216 | tf_op jit(solution)/shard_map/while/body/eval_jaxpr/hqk,qhe->khe/dot_general | solution.py:105
  460.9 13.2 %fusion.471 = f32[512,3,64]{0,2,1:T(8,128)} fusion(f32[3,512,1024]{2,1,0:T(8,128)} %fusion.468, f32[3,512,1024]{2,1,0:T(8,128)} %copy-done.1, f32[3,512]{1,0:T(4,128)S(1)} %get-tuple-element.521, bf16[2,1024,3,64]{1,3,2,0:T(8,128)(2,1)S(1)} %get-tuple-element.590, s32[]{:T(128)S(6)} %copy.134), kind=kOutput, calls=%fused_computation.116.clone.1.clone | convolution fusion | flops 215484928 | bytes 25968644 | tf_op jit(solution)/shard_map/while/body/eval_jaxpr/hqk,khe->qhe/dot_general | solution.py:103
  478.7 13.2 %fusion.474 = f32[512,3,64]{0,2,1:T(8,128)} fusion(f32[3,512,1024]{2,1,0:T(8,128)} %fusion.472, f32[3,512,1024]{2,1,0:T(8,128)} %copy-done.2, f32[3,512]{1,0:T(4,128)S(1)} %get-tuple-element.522, bf16[2,1024,3,64]{1,3,2,0:T(8,128)(2,1)S(1)} %get-tuple-element.590, s32[]{:T(128)S(6)} %copy.134), kind=kOutput, calls=%fused_computation.117.clone.1.clone | convolution fusion | flops 215484928 | bytes 25968644 | tf_op jit(solution)/shard_map/while/body/eval_jaxpr/hqk,khe->qhe/dot_general | solution.py:103
  491.9 14.1 %fusion.476 = f32[3,64,1024]{2,1,0:T(8,128)} fusion(f32[3,512,1024]{2,1,0:T(8,128)} %fusion.472, f32[3,512,1024]{2,1,0:T(8,128)} %copy-done.2, f32[3,512]{1,0:T(4,128)S(1)} %get-tuple-element.522, bf16[2,1024,3,64]{1,3,2,0:T(8,128)(2,1)S(1)} %get-tuple-element.591, s32[]{:T(128)S(6)} %copy.134), kind=kOutput, calls=%fused_computation.91.clone.1.clone | convolution fusion | flops 215484928 | bytes 26165252 | tf_op jit(solution)/shard_map/while/body/eval_jaxpr/hqk,qhe->khe/dot_general | solution.py:105
  506.0 14.3 %fusion.477 = f32[2,1024,3,64]{1,3,2,0:T(8,128)} fusion(f32[2,1024,3,64]{1,3,2,0:T(8,128)} %get-tuple-element.579, s32[]{:T(128)S(6)} %copy.134, f32[3,64,1024]{2,1,0:T(8,128)} %fusion.476, f32[3,512,1024]{2,1,0:T(8,128)} %fusion.468, f32[3,512,1024]{2,1,0:T(8,128)} %copy-done.1, f32[3,512]{1,0:T(4,128)S(1)} %get-tuple-element.521, ...), kind=kOutput, calls=%fused_computation.115.clone.1.clone | convolution fusion | flops 215681536 | bytes 26953216 | tf_op jit(solution)/shard_map/while/body/eval_jaxpr/hqk,qhe->khe/dot_general | solution.py:105
  545.1 6.2 convolution_convert_fusion.1
  552.6 9.0 convolution_convert_fusion.3
  561.8 7.6 fusion.316
  578.5 4.7 reduce-scatter.15.cloned.1.call-done
  593.7 30.0 %reduce-scatter.17.cloned.1.call-done = bf16[512,768]{1,0:T(8,128)(2,1)} async-done(((bf16[2048,768]{1,0:T(8,128)(2,1)}), bf16[512,768]{1,0:T(8,128)(2,1)}) %reduce-scatter.17.cloned.1.call-update) | async-done | bytes 786448 | tf_op jit(solution)/shard_map/reduce_scatter | solution.py:170
  626.3 10.3 %copy.88 = f32[512,6,768]{0,2,1:T(8,128)} copy(f32[512,6,768]{2,0,1:T(8,128)} %bitcast_dynamic-update-slice_fusion) | data formatting | bytes 18874368 | tf_op jit(solution)/shard_map/stack | solution.py:323
  639.1 8.7 convolution_convert_fusion
  647.8 12.7 %all-reduce.6 = (bf16[2,4608]{1,0:T(2,128)(2,1)}, bf16[768]{0:T(1024)(128)(2,1)}, bf16[768]{0:T(1024)(128)(2,1)}, bf16[768]{0:T(1024)(128)(2,1)}) all-reduce(bf16[2,4608]{1,0:T(2,128)(2,1)} %convolution_convert_fusion, bf16[768]{0:T(1024)(128)(2,1)} %get-tuple-element.194, ...), channel_id=1, replica_groups=mesh['wide'=8,'narrow'=4] {'narrow'}, use_global_device_ids=true, to_apply=%region_34.35 | all-reduce | flops 11520 | bytes 46080 | tf_op jit(solution)/shard_map/psum | solution.py:336
  671.5 40.9 %all-reduce.4 = (f32[4608]{0:T(1024)}, f32[768]{0:T(1024)}, f32[768]{0:T(1024)}, f32[768]{0:T(1024)}, f32[768]{0:T(1024)}) all-reduce(f32[4608]{0:T(1024)} %convert_reduce_fusion.3, bf16[768]{0:T(1024)(128)(2,1)} %get-tuple-element.248, bf16[768]{0:T(1024)(128)(2,1)} %get-tuple-element.249, ...), channel_id=1, replica_groups=mesh['wide'=8,'narrow'=4] {'wide'}, use_global_device_ids=true, to_apply=%region_38.39 | all-reduce | flops 7680 | bytes 56832 | tf_op jit(solution)/shard_map/psum | solution.py:365
  721.1 267.8 %all-reduce.9.cloned.1.call-done = (f32[1000,128]{1,0:T(8,128)}, f32[128,4608]{1,0:T(8,128)}, f32[3,768,192]{1,2,0:T(8,128)}, f32[192,768]{1,0:T(8,128)}, f32[768,768]{1,0:T(8,128)}, /*index=5*/f32[768,768]{1,0:T(8,128)}) async-done(((f32[1000,128]{1,0:T(8,128)}, f32[128,4608]{1,0:T(8,128)}, f32[3,768,192]{1,2,0:T(8,128)}, f32[192,768]{1,0:T(8,128)}, f32[768,768]{1,0:T(8,128)}, ...) | async-done | bytes 9949200 | tf_op jit(solution)/shard_map/psum | solution.py:365
  (430 shorter events, 327.1 us)
Async XLA Ops:
  7.2 247.2 %copy-start = (bf16[768,768]{1,0:T(8,128)(2,1)S(1)}, bf16[768,768]{1,0:T(8,128)(2,1)}, u32[]{:S(2)}) copy-start(bf16[768,768]{1,0:T(8,128)(2,1)} %param.33) | copy-start | bytes 3538948
  7.2 53.3 %all-gather.13.cloned.1.call-start = ((), (), s32[]{:S(2)}) async-start(), calls=%async_computation.11 | async-start | bytes 3932160 | tf_op jit(solution)/shard_map/all_gather | solution.py:144
  7.3 23.9 %copy-start.63 = (s32[512]{0:T(512)}, s32[512]{0:T(512)S(1)}, u32[]{:S(2)}) copy-start(s32[512]{0:T(512)S(1)} %add_select_fusion) | copy-start | bytes 6148
  8.7 17.0 %copy-start.73 = (f32[512]{0:T(512)}, f32[512]{0:T(512)S(1)}, u32[]{:S(2)}) copy-start(f32[512]{0:T(512)S(1)} %broadcast_multiply_fusion.3) | copy-start | bytes 6148
  10.2 15.5 %copy-start.81 = (f32[512]{0:T(512)}, f32[512]{0:T(512)S(1)}, u32[]{:S(2)}) copy-start(f32[512]{0:T(512)S(1)} %fusion.273) | copy-start | bytes 6148
  29.1 61.5 %all-gather.7.cloned.1.call-start = ((), (), s32[]{:S(2)}) async-start(), calls=%async_computation.6 | async-start | bytes 3932160 | tf_op jit(solution)/shard_map/all_gather | solution.py:144
  49.3 130.7 %reduce-scatter.11.cloned.1.call-start = ((), (), s32[]{:S(2)}) async-start(), calls=%async_computation.12 | async-start | bytes 3932160 | tf_op jit(solution)/shard_map/reduce_scatter | solution.py:153
  141.9 104.9 %all-gather.15.cloned.1.call-start = ((), (), s32[]{:S(2)}) async-start(), calls=%async_computation.13 | async-start | bytes 3932160 | tf_op jit(solution)/shard_map/all_gather | solution.py:166
  151.1 32.3 %copy-start.79 = (f32[768]{0:T(1024)S(1)}, f32[768]{0:T(1024)}, u32[]{:S(2)}) copy-start(f32[768]{0:T(1024)} %param.30) | copy-start | bytes 9220
  182.2 146.5 %copy-start.77 = (f32[512]{0:T(512)}, f32[512]{0:T(512)S(1)}, u32[]{:S(2)}) copy-start(f32[512]{0:T(512)S(1)} %broadcast_multiply_fusion.2) | copy-start | bytes 6148
  183.4 145.4 %copy-start.83 = (f32[512]{0:T(512)}, f32[512]{0:T(512)S(1)}, u32[]{:S(2)}) copy-start(f32[512]{0:T(512)S(1)} %fusion.274) | copy-start | bytes 6148
  184.7 69.6 %all-gather.11.cloned.1.call-start = ((), (), s32[]{:S(2)}) async-start(), calls=%async_computation.10 | async-start | bytes 3932160 | tf_op jit(solution)/shard_map/all_gather | solution.py:270
  185.6 146.8 %copy-start.75 = (f32[512]{0:T(512)}, f32[512]{0:T(512)S(1)}, u32[]{:S(2)}) copy-start(f32[512]{0:T(512)S(1)} %convert_element_type.185) | copy-start | bytes 6148
  191.9 92.6 %reduce-scatter.7.cloned.1.call-start = ((), (), s32[]{:S(2)}) async-start(), calls=%async_computation.7 | async-start | bytes 3932160 | tf_op jit(solution)/shard_map/reduce_scatter | solution.py:153
  246.4 78.6 %reduce-scatter.13.cloned.1.call-start = ((), (), s32[]{:S(2)}) async-start(), calls=%async_computation.14 | async-start | bytes 3932160 | tf_op jit(solution)/shard_map/reduce_scatter | solution.py:279
  254.3 14.5 %copy-start.98 = (bf16[768,768]{1,0:T(8,128)(2,1)S(1)}, bf16[768,768]{1,0:T(8,128)(2,1)}, u32[]{:S(2)}) copy-start(bf16[768,768]{1,0:T(8,128)(2,1)} %param.31) | copy-start | bytes 3538948
  272.9 90.7 %all-gather.17.cloned.1.call-start = ((), (), s32[]{:S(2)}) async-start(), calls=%async_computation.15 | async-start | bytes 3932160 | tf_op jit(solution)/shard_map/all_gather | solution.py:295
  286.5 38.5 %copy-start.6 = (f32[512,768]{1,0:T(8,128)S(1)}, f32[512,768]{1,0:T(8,128)}, u32[]{:S(2)}) copy-start(f32[512,768]{1,0:T(8,128)} %copy-done.5) | copy-start | bytes 4718596
  333.6 30.0 %copy-start.62 = (bf16[192,768]{1,0:T(8,128)(2,1)S(1)}, bf16[192,768]{1,0:T(8,128)(2,1)}, u32[]{:S(2)}) copy-start(bf16[192,768]{1,0:T(8,128)(2,1)} %param.29) | copy-start | bytes 884740
  334.9 216.6 %all-gather.9.cloned.1.call-start = ((), (), s32[]{:S(2)}) async-start(), calls=%async_computation.8 | async-start | bytes 3932160 | tf_op jit(solution)/shard_map/all_gather | solution.py:166
  335.6 247.6 %reduce-scatter.15.cloned.1.call-start = ((), (), s32[]{:S(2)}) async-start(), calls=%async_computation.16 | async-start | bytes 3932160 | tf_op jit(solution)/shard_map/reduce_scatter | solution.py:311
  545.1 78.6 %reduce-scatter.17.cloned.1.call-start = ((), (), s32[]{:S(2)}) async-start(), calls=%async_computation.17 | async-start | bytes 3932160 | tf_op jit(solution)/shard_map/reduce_scatter | solution.py:170
  551.4 164.7 %reduce-scatter.9.cloned.1.call-start = ((), (), s32[]{:S(2)}) async-start(), calls=%async_computation.9 | async-start | bytes 3932160 | tf_op jit(solution)/shard_map/reduce_scatter | solution.py:170
  561.7 427.2 %all-reduce.9.cloned.1.call-start = ((), (), s32[]{:S(2)}) async-start(), calls=%async_computation.18 | async-start | bytes 19898368 | tf_op jit(solution)/shard_map/psum | solution.py:365
  575.2 10.5 %copy-start.71 = (f32[768]{0:T(1024)S(1)}, f32[768]{0:T(1024)}, u32[]{:S(2)}) copy-start(f32[768]{0:T(1024)} %param.27) | copy-start | bytes 9220
  575.2 10.5 %copy-start.74 = (f32[512]{0:T(512)S(1)}, f32[512]{0:T(512)}, u32[]{:S(2)}) copy-start(f32[512]{0:T(512)} %copy-done.73) | copy-start | bytes 6148
  575.2 10.5 %copy-start.82 = (f32[512]{0:T(512)S(1)}, f32[512]{0:T(512)}, u32[]{:S(2)}) copy-start(f32[512]{0:T(512)} %copy-done.81) | copy-start | bytes 6148
  578.5 10.0 copy-start.19
  578.5 10.0 copy-start.76
  592.2 31.5 %copy-start.24 = (bf16[512,768]{1,0:T(8,128)(2,1)S(1)}, bf16[512,768]{1,0:T(8,128)(2,1)}, u32[]{:S(2)}) copy-start(bf16[512,768]{1,0:T(8,128)(2,1)} %param.35) | copy-start | bytes 2359300
  592.2 31.5 %copy-start.93 = (f32[768]{0:T(1024)S(1)}, f32[768]{0:T(1024)}, u32[]{:S(2)}) copy-start(f32[768]{0:T(1024)} %param.34) | copy-start | bytes 9220
  626.3 10.3 %copy-start.13 = (f32[512,1,768]{2,0,1:T(8,128)S(1)}, f32[512,1,768]{2,0,1:T(8,128)}, u32[]{:S(2)}) copy-start(f32[512,1,768]{2,0,1:T(8,128)} %copy.99) | copy-start | bytes 4718596
  (97 other events, 287.4 us)
Sparse Core Ops, SparseCore 0:
  29.2 31.2 all-gather.12
  62.0 28.5 all-gather.6
  142.1 37.9 reduce-scatter.10
  184.8 28.5 all-gather.14
  214.9 28.5 all-gather.10
  246.5 37.9 reduce-scatter.6
  287.0 37.9 reduce-scatter.12
  335.0 28.5 all-gather.16
  365.8 28.5 all-gather.8
  545.2 37.9 reduce-scatter.14
  585.7 37.9 reduce-scatter.16
  626.3 38.4 reduce-scatter.8
  671.2 317.7 all-reduce.8
where the time goes:
time: 1020 us; the launch traced here: 1010 us
  waiting for transfers between devices  417 us (41%)
  matrix products  295 us (29%)
  local copies, waits for them, and re-layouts  151 us (15%)
  other arithmetic  72.9 us (7%)
  blocking collectives  53.6 us (5%)
  between operations  15.1 us (1%)
    psum x1, waiting for transfers between devices, body(): lax.psum((grad_time_table, grad_w_ada, grad_b_ada, grad_gain_one, grad_w_...  268 us
    unnamed x211, local copies, waits for them, and re-layouts  67 us
    dot_general x4, matrix products, one_sequence(): jnp.einsum('hqk,qhe->khe', grad_scores, q_block, preferred_element_type=j...  56.8 us
    dot_general x4, matrix products, one_sequence(): jnp.einsum('hqk,khe->qhe', grad_scores, k_seq, preferred_element_type=jnp...  52.9 us
    psum x1, blocking collectives, body(): lax.psum((grad_time_table, grad_w_ada, grad_b_ada, grad_gain_one, grad_w_...  40.9 us
    reduce_scatter x1, waiting for transfers between devices, body(): lax.psum_scatter(jnp.einsum('tf,df->td', lax.slice_in_dim(grad_pre_low, 0...  36.5 us
    reduce_scatter x2, waiting for transfers between devices, forward(): lax.psum_scatter(jnp.dot(lax.slice_in_dim(heads_low, 0, tok_rows * lax.ax...  31.4 us
    reduce_scatter x2, waiting for transfers between devices, forward(): lax.psum_scatter(jnp.dot(lax.slice_in_dim(act_low, 0, tok_rows * lax.axis...  30 us
  transfers between devices with their start and end apart: 13, of which 9 were waited for; matrix products, arithmetic and copies ran while one was open for 40% of the time, Pallas kernels for 0%

commit v1 on v0

--- a/solution.py
+++ b/solution.py
@@ -235,11 +235,9 @@
         w_down,
         b_down,
     )
-    first_pass = forward(tokens, timestep, *weights)
-    again_inputs = lax.optimization_barrier((tokens,) + weights)
-    saved = forward(again_inputs[0], timestep, *again_inputs[1:])
+    saved = forward(tokens, timestep, *weights)
     (
-        unused_mixed,
+        mixed,
         step_pick,
         picked,
         cond_low,
@@ -338,48 +336,37 @@
         lax.psum(gain_two_part.astype(jnp.bfloat16), "narrow").astype(jnp.float32),
         lax.psum(b_down_part.astype(jnp.bfloat16), "narrow").astype(jnp.float32),
     )
-    grad_b_ada = jnp.sum(grad_modulation, axis=0)
-    modulation_low = grad_modulation.astype(jnp.bfloat16)
-    grad_w_ada = jnp.einsum(
-        "sc,sm->cm", cond_low, modulation_low, preferred_element_type=jnp.float32
-    )
+    all_modulation = lax.all_gather(grad_modulation, "wide", axis=0, tiled=True)
+    all_steps = lax.all_gather(timestep, "wide", axis=0, tiled=True)
+    all_pick = (
+        all_steps[:, None] == jnp.arange(time_table.shape[0], dtype=jnp.int32)[None, :]
+    ).astype(jnp.float32)
+    all_picked = jnp.dot(all_pick, time_table, precision=highest)
+    all_cond = jax.nn.silu(all_picked).astype(jnp.bfloat16)
+    grad_b_ada = jnp.sum(all_modulation, axis=0)
+    modulation_low = all_modulation.astype(jnp.bfloat16)
+    grad_w_ada = jnp.einsum("sc,sm->cm", all_cond, modulation_low, preferred_element_type=jnp.float32)
     grad_condition = jnp.einsum(
         "sm,cm->sc", modulation_low, w_ada, preferred_element_type=jnp.float32
     )
-    _, silu_pull = jax.vjp(jax.nn.silu, picked)
+    _, silu_pull = jax.vjp(jax.nn.silu, all_picked)
     grad_time_table = jnp.einsum(
-        "sn,sc->nc", step_pick, silu_pull(grad_condition)[0], precision=highest
-    )
-    (
-        grad_time_table,
-        grad_w_ada,
-        grad_b_ada,
-        grad_gain_one,
-        grad_w_qkv,
-        grad_w_out,
-        grad_gain_two,
-        grad_w_up,
-        grad_b_up,
-        grad_w_down,
-        grad_b_down,
-    ) = lax.psum(
-        (
-            grad_time_table,
-            grad_w_ada,
-            grad_b_ada,
-            grad_gain_one,
-            grad_w_qkv,
-            grad_w_out,
-            grad_gain_two,
-            grad_w_up,
-            grad_b_up,
-            grad_w_down,
-            grad_b_down,
-        ),
-        "wide",
-    )
+        "sn,sc->nc", all_pick, silu_pull(grad_condition)[0], precision=highest
+    )
+
+    def reduce_low(values):
+        return lax.psum(values.astype(jnp.bfloat16), "wide").astype(jnp.float32)
+
+    grad_gain_one = reduce_low(grad_gain_one)
+    grad_gain_two = reduce_low(grad_gain_two)
+    grad_b_up = reduce_low(grad_b_up)
+    grad_b_down = reduce_low(grad_b_down)
+    grad_w_qkv = reduce_low(grad_w_qkv)
+    grad_w_out = reduce_low(grad_w_out)
+    grad_w_up = reduce_low(grad_w_up)
+    grad_w_down = reduce_low(grad_w_down)
     return (
-        first_pass[0].astype(jnp.bfloat16),
+        mixed.astype(jnp.bfloat16),
         grad_tokens,
         grad_time_table,
         grad_w_ada,

time: 1020 us -> 836 us (0.82)
  local copies, waits for them, and re-layouts: 151 us -> 85.4 us
  waiting for transfers between devices: 417 us -> 352 us
  matrix products: 295 us -> 232 us
  blocking collectives: 53.6 us -> 78 us
    psum x1, waiting for transfers between devices: 268 us -> 119 us  [reduce_low(): return lax.psum(values.astype(jnp.bfloat16), 'wide').astype(jnp.float32)]
    unnamed x211 -> x183, local copies, waits for them, and re-layouts: 67 us -> 33.3 us
    all_gather x0 -> x1, blocking collectives: none -> 30.9 us  [body(): all_modulation = lax.all_gather(grad_modulation, 'wide', axis=0, tiled=True)]
    all_gather x1, waiting for transfers between devices: 0.01 us -> 28.6 us  [body(): lax.all_gather(grad_branch.astype(jnp.bfloat16), 'narrow', axis=0, tiled=...]
    all_gather x2 -> x1, waiting for transfers between devices: 0.04 us -> 28.4 us  [forward(): lax.all_gather(normed_two_low, 'narrow', axis=0, tiled=True)]
    reduce_scatter x1, waiting for transfers between devices: 4.74 us -> 31.7 us  [body(): lax.psum_scatter(jnp.einsum('kte,kde->td', grad_projected, w_qkv, preferr...]
    sub x4 -> x0, matrix products: 25 us -> none  [one_sequence(): exp_scores = jnp.exp(scores - row_max)]
    psum x1, blocking collectives: 40.9 us -> 22.5 us  [reduce_low(): return lax.psum(values.astype(jnp.bfloat16), 'wide').astype(jnp.float32)]
  transfers between devices with their start and end apart: 13 -> 9, of which waited for: 9 -> 9; matrix products, arithmetic and copies ran while one was open for 40% -> 5% of each run, Pallas kernels for 0% -> 0%
where the time goes in v1:
time: 836 us; the launch traced here: 829 us
  waiting for transfers between devices  352 us (42%)
  matrix products  232 us (28%)
  local copies, waits for them, and re-layouts  85.4 us (10%)
  blocking collectives  78 us (9%)
  other arithmetic  63.3 us (8%)
  between operations  15.8 us (2%)
    psum x1, waiting for transfers between devices, reduce_low(): return lax.psum(values.astype(jnp.bfloat16), 'wide').astype(jnp.float32)  119 us
    dot_general x4, matrix products, one_sequence(): jnp.einsum('hqk,qhe->khe', grad_scores, q_block, preferred_element_type=j...  56.7 us
    dot_general x4, matrix products, one_sequence(): jnp.einsum('hqk,khe->qhe', grad_scores, k_seq, preferred_element_type=jnp...  56.3 us
    reduce_scatter x1, waiting for transfers between devices, body(): lax.psum_scatter(jnp.einsum('tf,df->td', lax.slice_in_dim(grad_pre_low, 0...  38.1 us
    reduce_scatter x1, waiting for transfers between devices, forward(): lax.psum_scatter(jnp.dot(lax.slice_in_dim(act_low, 0, tok_rows * lax.axis...  34.3 us
    unnamed x183, local copies, waits for them, and re-layouts  33.3 us
    reduce_scatter x1, waiting for transfers between devices, body(): lax.psum_scatter(jnp.einsum('kte,kde->td', grad_projected, w_qkv, preferr...  31.7 us
    all_gather x1, blocking collectives, body(): all_modulation = lax.all_gather(grad_modulation, 'wide', axis=0, tiled=True)  30.9 us
  transfers between devices with their start and end apart: 9, of which 9 were waited for; matrix products, arithmetic and copies ran while one was open for 5% of the time, Pallas kernels for 0%

profile of v1, /device:TPU:0, one launch (start us, length us, event | category | flops | bytes accessed | tf_op | source)
XLA Modules:
  0.0 828.8 jit_solution(5324140804440143015)
XLA Ops:
  33.1 27.6 %all-gather.6.cloned.1.call-done = bf16[2048,768]{1,0:T(8,128)(2,1)} async-done(((bf16[512,768]{1,0:T(8,128)(2,1)}), bf16[2048,768]{1,0:T(8,128)(2,1)}) %all-gather.6.cloned.1.call-update) | async-done | bytes 3145744 | tf_op jit(solution)/shard_map/all_gather | solution.py:144
  81.2 20.5 %while.28 = (s32[]{:T(128)}, bf16[2,1024,3,64]{1,3,2,0:T(8,128)(2,1)}, f32[2,3,1024]{2,1,0:T(4,128)}, bf16[2,1024,3,64]{1,3,2,0:T(8,128)(2,1)S(1)}, bf16[2,1024,...) while((s32[]{:T(128)}, bf16[2,1024,3,64]{1,3,2,0:T(8,128)(2,1)}, ...), condition=%wide.region_7.8_spmd.clone, body=%wide.region_2.7_spmd.sunk.clone | while | flops 834404352 | bytes 47524568 | solution.py:73
  115.8 30.3 %reduce-scatter.5.cloned.1.call-done = bf16[512,768]{1,0:T(8,128)(2,1)} async-done(((bf16[2048,768]{1,0:T(8,128)(2,1)}), bf16[512,768]{1,0:T(8,128)(2,1)}) %reduce-scatter.5.cloned.1.call-update) | async-done | bytes 786448 | tf_op jit(solution)/shard_map/reduce_scatter | solution.py:153
  150.6 28.4 %all-gather.8.cloned.1.call-done = bf16[2048,768]{1,0:T(8,128)(2,1)} async-done(((bf16[512,768]{1,0:T(8,128)(2,1)}), bf16[2048,768]{1,0:T(8,128)(2,1)}) %all-gather.8.cloned.1.call-update) | async-done | bytes 3145744 | tf_op jit(solution)/shard_map/all_gather | solution.py:166
  179.0 4.9 fusion.228
  186.5 5.4 convolution_convert_fusion.2
  195.8 34.3 %reduce-scatter.7.cloned.1.call-done = bf16[512,768]{1,0:T(8,128)(2,1)} async-done(((bf16[2048,768]{1,0:T(8,128)(2,1)}), bf16[512,768]{1,0:T(8,128)(2,1)}) %reduce-scatter.7.cloned.1.call-update) | async-done | bytes 786448 | tf_op jit(solution)/shard_map/reduce_scatter | solution.py:170
  234.2 28.6 %all-gather.10.cloned.1.call-done = bf16[2048,768]{1,0:T(8,128)(2,1)} async-done(((bf16[512,768]{1,0:T(8,128)(2,1)}), bf16[2048,768]{1,0:T(8,128)(2,1)}) %all-gather.10.cloned.1.call-update) | async-done | bytes 3145744 | tf_op jit(solution)/shard_map/all_gather | solution.py:268
  262.9 10.9 %fusion.215 = (bf16[768]{0:T(1024)(128)(2,1)}, bf16[2048,768]{1,0:T(8,128)(2,1)S(1)}) fusion(f32[2048,768]{1,0:T(8,128)} %copy-done.93, f32[768]{0:T(1024)} %param.30, bf16[2048,768]{1,0:T(8,128)(2,1)} %all-gather.10.cloned.1.call-done, bf16[768,768]{1,0:T(8,128)(2,1)S(1)} %copy-done), kind=kOutput, calls=%fused_computation.265 | convolution fusion | flops 2450521344 | bytes 13767168 | tf_op jit(solution)/shard_map/td,fd->tf/dot_general | solution.py:270
  279.5 38.1 %reduce-scatter.9.cloned.1.call-done = bf16[512,768]{1,0:T(8,128)(2,1)} async-done(((bf16[2048,768]{1,0:T(8,128)(2,1)}), bf16[512,768]{1,0:T(8,128)(2,1)}) %reduce-scatter.9.cloned.1.call-update) | async-done | bytes 786448 | tf_op jit(solution)/shard_map/reduce_scatter | solution.py:277
  324.3 6.7 convolution_convert_fusion.6
  331.0 7.8 convolution_convert_fusion.5
  338.9 13.7 %all-gather.12.cloned.1.call-done = bf16[2048,768]{1,0:T(8,128)(2,1)} async-done(((bf16[512,768]{1,0:T(8,128)(2,1)}), bf16[2048,768]{1,0:T(8,128)(2,1)}) %all-gather.12.cloned.1.call-update) | async-done | bytes 3145744 | tf_op jit(solution)/shard_map/all_gather | solution.py:293
  360.3 149.3 %while.29 = (s32[]{:T(128)}, f32[2,1024,3,64]{1,3,2,0:T(8,128)}, f32[2,1024,3,64]{1,3,2,0:T(8,128)}, bf16[2,1024,3,64]{1,3,2,0:T(8,128)(2,1)}, bf16[2,1024,3,64]...) while((s32[]{:T(128)}, f32[2,1024,3,64]{1,3,2,0:T(8,128)}, ...), condition=%wide.region_18.19_spmd.clone, body=%wide.region_15.18_spmd.sunk.clone | while | flops 2079926272 | bytes 209329936 | solution.py:110
  372.8 14.0 %fusion.347 = f32[512,3,64]{0,2,1:T(8,128)S(1)} fusion(f32[3,512,1024]{2,1,0:T(8,128)} %fusion.344, f32[3,512,1024]{2,1,0:T(8,128)} %copy-done.2, f32[3,512]{1,0:T(4,128)S(1)} %get-tuple-element.382, bf16[2,1024,3,64]{1,3,2,0:T(8,128)(2,1)S(1)} %get-tuple-element.436, s32[]{:T(128)S(6)} %copy.116), kind=kOutput, calls=%fused_computation.72.clone.1.clone | convolution fusion | flops 215484928 | bytes 25968644 | tf_op jit(solution)/shard_map/while/body/eval_jaxpr/hqk,khe->qhe/dot_general | solution.py:103
  386.8 4.6 fusion.348
  391.4 14.2 %fusion.350 = f32[512,3,64]{0,2,1:T(8,128)S(1)} fusion(f32[3,512,1024]{2,1,0:T(8,128)} %fusion.348, f32[3,512,1024]{2,1,0:T(8,128)} %copy-done.3, f32[3,512]{1,0:T(4,128)S(1)} %get-tuple-element.383, bf16[2,1024,3,64]{1,3,2,0:T(8,128)(2,1)S(1)} %get-tuple-element.436, s32[]{:T(128)S(6)} %copy.116), kind=kOutput, calls=%fused_computation.73.clone.1.clone | convolution fusion | flops 215484928 | bytes 25968644 | tf_op jit(solution)/shard_map/while/body/eval_jaxpr/hqk,khe->qhe/dot_general | solution.py:103
  405.6 14.1 %fusion.352 = f32[3,64,1024]{2,1,0:T(8,128)} fusion(f32[3,512,1024]{2,1,0:T(8,128)} %fusion.348, f32[3,512,1024]{2,1,0:T(8,128)} %copy-done.3, f32[3,512]{1,0:T(4,128)S(1)} %get-tuple-element.383, bf16[2,1024,3,64]{1,3,2,0:T(8,128)(2,1)S(1)} %get-tuple-element.437, s32[]{:T(128)S(6)} %copy.116), kind=kOutput, calls=%fused_computation.47.clone.1.clone | convolution fusion | flops 215484928 | bytes 26165252 | tf_op jit(solution)/shard_map/while/body/eval_jaxpr/hqk,qhe->khe/dot_general | solution.py:105
  419.7 14.3 %fusion.353 = f32[2,1024,3,64]{1,3,2,0:T(8,128)} fusion(f32[2,1024,3,64]{1,3,2,0:T(8,128)} %get-tuple-element.425, s32[]{:T(128)S(6)} %copy.116, f32[3,64,1024]{2,1,0:T(8,128)} %fusion.352, f32[3,512,1024]{2,1,0:T(8,128)} %fusion.344, f32[3,512,1024]{2,1,0:T(8,128)} %copy-done.2, f32[3,512]{1,0:T(4,128)S(1)} %get-tuple-element.382, ...), kind=kOutput, calls=%fused_computation.71.clone.1.clone | convolution fusion | flops 215681536 | bytes 26953216 | tf_op jit(solution)/shard_map/while/body/eval_jaxpr/hqk,qhe->khe/dot_general | solution.py:105
  447.3 14.0 %fusion.347 = f32[512,3,64]{0,2,1:T(8,128)S(1)} fusion(f32[3,512,1024]{2,1,0:T(8,128)} %fusion.344, f32[3,512,1024]{2,1,0:T(8,128)} %copy-done.2, f32[3,512]{1,0:T(4,128)S(1)} %get-tuple-element.382, bf16[2,1024,3,64]{1,3,2,0:T(8,128)(2,1)S(1)} %get-tuple-element.436, s32[]{:T(128)S(6)} %copy.116), kind=kOutput, calls=%fused_computation.72.clone.1.clone | convolution fusion | flops 215484928 | bytes 25968644 | tf_op jit(solution)/shard_map/while/body/eval_jaxpr/hqk,khe->qhe/dot_general | solution.py:103
  461.2 4.6 fusion.348
  465.9 14.2 %fusion.350 = f32[512,3,64]{0,2,1:T(8,128)S(1)} fusion(f32[3,512,1024]{2,1,0:T(8,128)} %fusion.348, f32[3,512,1024]{2,1,0:T(8,128)} %copy-done.3, f32[3,512]{1,0:T(4,128)S(1)} %get-tuple-element.383, bf16[2,1024,3,64]{1,3,2,0:T(8,128)(2,1)S(1)} %get-tuple-element.436, s32[]{:T(128)S(6)} %copy.116), kind=kOutput, calls=%fused_computation.73.clone.1.clone | convolution fusion | flops 215484928 | bytes 25968644 | tf_op jit(solution)/shard_map/while/body/eval_jaxpr/hqk,khe->qhe/dot_general | solution.py:103
  480.1 14.1 %fusion.352 = f32[3,64,1024]{2,1,0:T(8,128)} fusion(f32[3,512,1024]{2,1,0:T(8,128)} %fusion.348, f32[3,512,1024]{2,1,0:T(8,128)} %copy-done.3, f32[3,512]{1,0:T(4,128)S(1)} %get-tuple-element.383, bf16[2,1024,3,64]{1,3,2,0:T(8,128)(2,1)S(1)} %get-tuple-element.437, s32[]{:T(128)S(6)} %copy.116), kind=kOutput, calls=%fused_computation.47.clone.1.clone | convolution fusion | flops 215484928 | bytes 26165252 | tf_op jit(solution)/shard_map/while/body/eval_jaxpr/hqk,qhe->khe/dot_general | solution.py:105
  494.1 14.3 %fusion.353 = f32[2,1024,3,64]{1,3,2,0:T(8,128)} fusion(f32[2,1024,3,64]{1,3,2,0:T(8,128)} %get-tuple-element.425, s32[]{:T(128)S(6)} %copy.116, f32[3,64,1024]{2,1,0:T(8,128)} %fusion.352, f32[3,512,1024]{2,1,0:T(8,128)} %fusion.344, f32[3,512,1024]{2,1,0:T(8,128)} %copy-done.2, f32[3,512]{1,0:T(4,128)S(1)} %get-tuple-element.382, ...), kind=kOutput, calls=%fused_computation.71.clone.1.clone | convolution fusion | flops 215681536 | bytes 26953216 | tf_op jit(solution)/shard_map/while/body/eval_jaxpr/hqk,qhe->khe/dot_general | solution.py:105
  534.9 13.1 %all-reduce.4 = s32[16]{0:T(128)S(1)} all-reduce(s32[16]{0:T(128)S(1)} %dynamic-update-slice), channel_id=1, replica_groups=mesh['wide'=8,'narrow'=4] {'wide'}, use_global_device_ids=true, to_apply=%add.4 | all-reduce | flops 16 | bytes 128
  548.3 119.3 %all-reduce.10.cloned.1.call-done = (bf16[3,768,192]{1,2,0:T(8,128)(2,1)}, bf16[192,768]{1,0:T(8,128)(2,1)}, bf16[768,768]{1,0:T(8,128)(2,1)}, bf16[768,768]{1,0:T(8,128)(2,1)}) async-done(((bf16[3,768,192]{1,2,0:T(8,128)(2,1)}, bf16[192,768]{1,0:T(8,128)(2,1)}, bf16[768,768]{1,0:T(8,128)(2,1)}, bf16[768,768]{1,0:T(8,128)(2,1)}), (bf16[3,768,192]{1,2,0:T(8,128)(2,1)}, bf16[192,768]{1,0:T(8,128)(2,1)}, ...) | async-done | bytes 3538960 | tf_op jit(solution)/shard_map/psum | solution.py:358
  675.3 31.7 %reduce-scatter.11.cloned.1.call-done = bf16[512,768]{1,0:T(8,128)(2,1)} async-done(((bf16[2048,768]{1,0:T(8,128)(2,1)}), bf16[512,768]{1,0:T(8,128)(2,1)}) %reduce-scatter.11.cloned.1.call-update) | async-done | bytes 786448 | tf_op jit(solution)/shard_map/reduce_scatter | solution.py:309
  720.9 9.6 %copy.87 = f32[512,6,768]{0,2,1:T(8,128)} copy(f32[512,6,768]{2,0,1:T(8,128)} %bitcast_dynamic-update-slice_fusion) | data formatting | bytes 18874368 | tf_op jit(solution)/shard_map/stack | solution.py:321
  730.5 8.8 %convolution_convert_fusion = bf16[2,4608]{1,0:T(2,128)(2,1)} fusion(f32[512,4608]{0,1:T(8,128)} %bitcast.318, s32[512]{0:T(512)S(1)} %copy-done.56), kind=kOutput, calls=%fused_computation.129 | convolution fusion | flops 56634368 | bytes 9457664 | tf_op jit(solution)/shard_map/ts,tm->sm/dot_general | solution.py:332
  739.4 11.6 %all-reduce.7 = (bf16[2,4608]{1,0:T(2,128)(2,1)}, bf16[768]{0:T(1024)(128)(2,1)}, bf16[768]{0:T(1024)(128)(2,1)}, bf16[768]{0:T(1024)(128)(2,1)}) all-reduce(bf16[2,4608]{1,0:T(2,128)(2,1)} %convolution_convert_fusion, bf16[768]{0:T(1024)(128)(2,1)} %get-tuple-element.147, ...), channel_id=1, replica_groups=mesh['wide'=8,'narrow'=4] {'narrow'}, use_global_device_ids=true, to_apply=%region_22.23 | all-reduce | flops 11520 | bytes 46080 | tf_op jit(solution)/shard_map/psum | solution.py:334
  750.9 22.5 %all-reduce.5 = (bf16[768]{0:T(1024)(128)(2,1)}, bf16[768]{0:T(1024)(128)(2,1)}, bf16[768]{0:T(1024)(128)(2,1)}, bf16[768]{0:T(1024)(128)(2,1)}) all-reduce(bf16[768]{0:T(1024)(128)(2,1)} %get-tuple-element.188, bf16[768]{0:T(1024)(128)(2,1)} %get-tuple-element.189, ...), channel_id=1, replica_groups=mesh['wide'=8,'narrow'=4] {'wide'}, use_global_device_ids=true, to_apply=%region_26.27 | all-reduce | flops 3072 | bytes 12288 | tf_op jit(solution)/shard_map/psum | solution.py:358
  779.2 30.9 %all-gather = f32[8,2,4608]{2,1,0:T(2,128)S(1)} all-gather(f32[1,2,4608]{2,1,0:T(2,128)S(1)} %bitcast_convert_fusion.1), channel_id=1, replica_groups=mesh['wide'=8,'narrow'=4] {'wide'}, dimensions={0}, use_global_device_ids=true | all-gather | bytes 331776 | tf_op jit(solution)/shard_map/all_gather | solution.py:339
  (357 shorter events, 205.6 us)
Async XLA Ops:
  7.2 179.4 %copy-start = (bf16[768,768]{1,0:T(8,128)(2,1)S(1)}, bf16[768,768]{1,0:T(8,128)(2,1)}, u32[]{:S(2)}) copy-start(bf16[768,768]{1,0:T(8,128)(2,1)} %param.31) | copy-start | bytes 3538948
  7.2 53.5 %all-gather.6.cloned.1.call-start = ((), (), s32[]{:S(2)}) async-start(), calls=%async_computation.4 | async-start | bytes 3932160 | tf_op jit(solution)/shard_map/all_gather | solution.py:144
  8.7 17.8 %copy-start.60 = (f32[512]{0:T(512)}, f32[512]{0:T(512)S(1)}, u32[]{:S(2)}) copy-start(f32[512]{0:T(512)S(1)} %broadcast_multiply_fusion.3) | copy-start | bytes 6148
  10.2 16.3 %copy-start.70 = (f32[512]{0:T(512)}, f32[512]{0:T(512)S(1)}, u32[]{:S(2)}) copy-start(f32[512]{0:T(512)S(1)} %fusion.206) | copy-start | bytes 6148
  29.3 31.4 %copy-start.87 = (bf16[3,768,192]{1,2,0:T(8,128)(2,1)S(1)}, bf16[3,768,192]{1,2,0:T(8,128)(2,1)}, u32[]{:S(2)}) copy-start(bf16[3,768,192]{1,2,0:T(8,128)(2,1)} %param.26) | copy-start | bytes 2654212
  29.3 116.8 %reduce-scatter.5.cloned.1.call-start = ((), (), s32[]{:S(2)}) async-start(), calls=%async_computation.5 | async-start | bytes 3932160 | tf_op jit(solution)/shard_map/reduce_scatter | solution.py:153
  108.0 71.0 %all-gather.8.cloned.1.call-start = ((), (), s32[]{:S(2)}) async-start(), calls=%async_computation.6 | async-start | bytes 3932160 | tf_op jit(solution)/shard_map/all_gather | solution.py:166
  115.8 33.0 %copy-start.68 = (f32[768]{0:T(1024)S(1)}, f32[768]{0:T(1024)}, u32[]{:S(2)}) copy-start(f32[768]{0:T(1024)} %param.28) | copy-start | bytes 9220
  148.4 172.2 %copy-start.4 = (f32[512,768]{1,0:T(8,128)}, f32[512,768]{1,0:T(8,128)S(1)}, u32[]{:S(2)}) copy-start(f32[512,768]{1,0:T(8,128)S(1)} %get-tuple-element.198) | copy-start | bytes 4718596
  148.4 172.2 %copy-start.62 = (f32[512]{0:T(512)}, f32[512]{0:T(512)S(1)}, u32[]{:S(2)}) copy-start(f32[512]{0:T(512)S(1)} %broadcast_multiply_fusion.2) | copy-start | bytes 6148
  148.9 171.7 %copy-start.72 = (f32[512]{0:T(512)}, f32[512]{0:T(512)S(1)}, u32[]{:S(2)}) copy-start(f32[512]{0:T(512)S(1)} %fusion.207) | copy-start | bytes 6148
  150.3 79.8 %reduce-scatter.7.cloned.1.call-start = ((), (), s32[]{:S(2)}) async-start(), calls=%async_computation.7 | async-start | bytes 3932160 | tf_op jit(solution)/shard_map/reduce_scatter | solution.py:170
  150.5 36.0 %copy-start.89 = (f32[768]{0:T(1024)S(1)}, f32[768]{0:T(1024)}, u32[]{:S(2)}) copy-start(f32[768]{0:T(1024)} %param.30) | copy-start | bytes 9220
  192.0 70.9 %all-gather.10.cloned.1.call-start = ((), (), s32[]{:S(2)}) async-start(), calls=%async_computation.8 | async-start | bytes 3932160 | tf_op jit(solution)/shard_map/all_gather | solution.py:268
  192.7 128.7 %copy-start.64 = (f32[512]{0:T(512)}, f32[512]{0:T(512)S(1)}, u32[]{:S(2)}) copy-start(f32[512]{0:T(512)S(1)} %convert_element_type.178) | copy-start | bytes 6148
  234.2 83.4 %reduce-scatter.9.cloned.1.call-start = ((), (), s32[]{:S(2)}) async-start(), calls=%async_computation.9 | async-start | bytes 3932160 | tf_op jit(solution)/shard_map/reduce_scatter | solution.py:277
  262.9 12.6 %copy-start.86 = (bf16[768,768]{1,0:T(8,128)(2,1)S(1)}, bf16[768,768]{1,0:T(8,128)(2,1)}, u32[]{:S(2)}) copy-start(bf16[768,768]{1,0:T(8,128)(2,1)} %param.29) | copy-start | bytes 3538948
  279.4 41.1 %copy-start.80 = (f32[512]{0:T(512)S(1)}, f32[512]{0:T(512)}, u32[]{:S(2)}) copy-start(f32[512]{0:T(512)} %copy-done.79) | copy-start | bytes 6148
  279.5 73.1 %all-gather.12.cloned.1.call-start = ((), (), s32[]{:S(2)}) async-start(), calls=%async_computation.10 | async-start | bytes 3932160 | tf_op jit(solution)/shard_map/all_gather | solution.py:293
  323.8 343.8 %all-reduce.10.cloned.1.call-start = ((), (), s32[]{:S(2)}) async-start(), calls=%async_computation.12 | async-start | bytes 7077888 | tf_op jit(solution)/shard_map/psum | solution.py:358
  331.0 21.5 %copy-start.52 = (bf16[192,768]{1,0:T(8,128)(2,1)S(1)}, bf16[192,768]{1,0:T(8,128)(2,1)}, u32[]{:S(2)}) copy-start(bf16[192,768]{1,0:T(8,128)(2,1)} %param.27) | copy-start | bytes 884740
  526.9 180.2 %reduce-scatter.11.cloned.1.call-start = ((), (), s32[]{:S(2)}) async-start(), calls=%async_computation.11 | async-start | bytes 3932160 | tf_op jit(solution)/shard_map/reduce_scatter | solution.py:309
  532.7 15.2 %copy-start.48 = (f32[1000,128]{1,0:T(8,128)S(1)}, f32[1000,128]{1,0:T(8,128)}, u32[]{:S(2)}) copy-start(f32[1000,128]{1,0:T(8,128)} %param.22) | copy-start | bytes 1536004
  548.0 124.1 %copy-start.82 = (s32[16]{0:T(128)}, s32[16]{0:T(128)S(1)}, u32[]{:S(2)}) copy-start(s32[16]{0:T(128)S(1)} %all-reduce.4) | copy-start | bytes 196
  672.1 34.9 %copy-start.7 = (bf16[512,768]{1,0:T(8,128)(2,1)S(1)}, bf16[512,768]{1,0:T(8,128)(2,1)}, u32[]{:S(2)}) copy-start(bf16[512,768]{1,0:T(8,128)(2,1)} %param.19) | copy-start | bytes 2359300
  672.1 34.9 %copy-start.14 = (f32[512,1,768]{2,0,1:T(8,128)S(1)}, f32[512,1,768]{2,0,1:T(8,128)}, u32[]{:S(2)}) copy-start(f32[512,1,768]{2,0,1:T(8,128)} %copy-done.13) | copy-start | bytes 4718596
  672.1 34.9 %copy-start.61 = (f32[512]{0:T(512)S(1)}, f32[512]{0:T(512)}, u32[]{:S(2)}) copy-start(f32[512]{0:T(512)} %copy-done.60) | copy-start | bytes 6148
  672.2 34.9 %copy-start.67 = (f32[768]{0:T(1024)S(1)}, f32[768]{0:T(1024)}, u32[]{:S(2)}) copy-start(f32[768]{0:T(1024)} %param.25) | copy-start | bytes 9220
  672.2 34.9 %copy-start.71 = (f32[512]{0:T(512)S(1)}, f32[512]{0:T(512)}, u32[]{:S(2)}) copy-start(f32[512]{0:T(512)} %copy-done.70) | copy-start | bytes 6148
  673.8 35.8 %copy-start.78 = (f32[512]{0:T(512)S(1)}, f32[512]{0:T(512)}, u32[]{:S(2)}) copy-start(f32[512]{0:T(512)} %copy-done.77) | copy-start | bytes 6148
  730.5 82.6 %copy-start.38 = (bf16[128,4608]{1,0:T(8,128)(2,1)S(1)}, bf16[128,4608]{1,0:T(8,128)(2,1)}, u32[]{:S(2)}) copy-start(bf16[128,4608]{1,0:T(8,128)(2,1)} %param.23) | copy-start | bytes 3538948
  739.4 80.2 %copy-start.76 = (f32[512]{0:T(512)S(1)}, f32[512]{0:T(512)}, u32[]{:S(2)}) copy-start(f32[512]{0:T(512)} %copy-done.74) | copy-start | bytes 6148
  (80 other events, 265.5 us)
Sparse Core Ops, SparseCore 0:
  29.4 31.2 all-gather.5
  108.1 37.9 reduce-scatter.4
  150.4 28.5 all-gather.7
  192.1 37.9 reduce-scatter.6
  234.3 28.5 all-gather.9
  279.6 37.9 reduce-scatter.8
  324.0 28.5 all-gather.11
  527.0 140.5 all-reduce.9
  670.1 36.8 reduce-scatter.10

commit v2 on v1

v2 whole, which is shorter than its diff:
```python
import functools
import math

import jax
import jax.numpy as jnp
import numpy as np
from jax import lax
from jax.experimental import pallas as pl
from jax.experimental.pallas import tpu as pltpu
from jax.sharding import PartitionSpec as P

D = 768
HD = 64
LEN = 1024
ROWS_LOCAL = 512
SHARD_HEADS = 3
QKV_ROWS = 576
GRAD_ROWS = 2304
MESH = pl.DeviceIdType.MESH
f32 = jnp.float32
bf16 = jnp.bfloat16
norm_eps = 1e-06
highest = lax.Precision.HIGHEST

NN = (((1,), (0,)), ((), ()))
NT = (((1,), (1,)), ((), ()))
TN = (((0,), (0,)), ((), ()))

CHUNKS = {
    "d0": (0, 192),
    "d1": (192, 192),
    "d2": (384, 192),
    "d3": (576, 192),
    "u0": (768, 192),
    "u1": (960, 192),
    "u2": (1152, 192),
    "u3": (1344, 192),
    "o": (1536, 192),
    "q": (1728, 192),
    "k": (1920, 192),
    "v": (2112, 192),
}
ORDERS = {
    "d0": (1, 0, "y", 2),
    "d1": (1, 0, "y", 2),
    "d2": (0, 1, "y", 2),
    "d3": ("y", 0, 1, 2),
    "u0": ("y", 0, 1, 2),
    "u1": (0, 1, "y", 2),
    "u2": (0, 1, "y", 2),
    "u3": ("y", 0, 1, 2),
    "o": (0, 1, "y", 2),
    "q": (0, "y", 1, 2),
    "k": ("y", 0, 1, 2),
    "v": ("y", 1, 0, 2),
}
PIECES = {
    "q": (0, 1, 0, 1, 0, 1,),
    "o": (0,),
    "u": (1, 0, 1, 0,),
    "d": (1, 0, 1, 0,),
}
PLACES = (
    "n0", "n1", "p0", "p1", "a0", "a1", "a2", "wq", "p2", "p3", "a3", "a4", "a5", "wo", "o0", "o1", "u3",
    "wu", "u4", "u5", "u6", "u7", "f0", "f1", "f2", "wd", "f3", "f4", "f5", "f6", "f7", "f8", "h0", "h1",
    "h2", "b0", "b1", "b2", "bx", "b3", "b4", "b5", "by", "g0", "g1", "g2", "g3",
)
SCHEDULE = {
    "n1": (
        "Wq0",
    ),
    "p0": (
        "Wq1",
    ),
    "a0": (
        "Wq2",
    ),
    "a1": (
        "Wq3",
    ),
    "a2": (
        "Wq4", "Wq5",
    ),
    "p2": (
        "Wo0",
    ),
    "a3": (
        "Wu0",
    ),
    "a5": (
        "Wu1",
    ),
    "o1": (
        "Wu2",
    ),
    "u3": (
        "Wu3", "Wd0",
    ),
    "u4": (
        "Wd1",
    ),
    "u5": (
        "Wd2",
    ),
    "f0": (
        "Wd3", "d3",
    ),
    "f1": (
        "d2", "d1", "d0",
    ),
    "f4": (
        "u0", "u3", "d3",
    ),
    "f5": (
        "u2", "u1", "d1",
    ),
    "f6": (
        "d2",
    ),
    "f7": (
        "u0", "d3", "d0",
    ),
    "f8": (
        "d2",
    ),
    "h0": (
        "u2", "d3",
    ),
    "h1": (
        "u3", "o",
    ),
    "b0": (
        "d2", "u2", "re", "u1",
    ),
    "b1": (
        "u2", "re", "d3", "d1",
    ),
    "b2": (
        "d2", "u0", "u1", "d1",
    ),
    "bx": (
        "k", "v", "d0", "u2", "d3",
    ),
    "b3": (
        "d2", "u0", "u3", "u1",
    ),
    "b4": (
        "u2", "d1", "o", "re",
    ),
    "b5": (
        "u0", "u3", "d3",
    ),
    "by": (
        "k", "u1", "q", "o",
    ),
    "g0": (
        "d2", "re", "u0", "v", "d0",
    ),
    "g1": (
        "u2", "u3", "u1", "o", "d1",
    ),
    "g2": (
        "re", "rl",
    ),
    "g3": (
        "k", "v", "re", "rl", "d0", "u3", "q", "o", "d1", "u0", "k", "q", "o", "u1", "v", "rl", "k", "q", "d0",
        "rl", "v", "u3", "k", "o", "q", "v", "d0", "rl", "q", "k", "rl", "v", "q",
    ),
}


def chunk_stages(name, n_bits):
    rows = CHUNKS[name][1]
    out = []
    before_y = True
    order = [dim for dim in ORDERS[name] if dim == "y" or dim < n_bits]
    for dim in order + list(range(3, n_bits)):
        if dim == "y":
            out.append((dim, False, rows, False))
            before_y = False
        else:
            halved = rows % 32 == 0
            rows = rows // 2 if halved else rows
            out.append((dim, halved, rows, before_y))
    return out


def stage_rows(index, n_bits):
    total = 0
    for name in CHUNKS:
        _, _, rows, both = chunk_stages(name, n_bits)[index]
        total += 2 * rows if both else rows
    return total


def outbox_rows(n_bits):
    return sum(rows for name in CHUNKS for _, halved, rows, both in chunk_stages(name, n_bits) if halved and both)


def dot(left, right, dims):
    return lax.dot_general(left, right, dims, preferred_element_type=f32)


def loop(count, body):
    def step(index, carry):
        body(index)
        return carry

    lax.fori_loop(0, count, step, 0)


def rows_at(offset, size, align):
    if isinstance(offset, int):
        return pl.ds(offset, size)
    return pl.ds(pl.multiple_of(offset, align), size)


def normalize(values):
    centered = values - jnp.mean(values, axis=-1, keepdims=True)
    variance = jnp.mean(centered * centered, axis=-1, keepdims=True)
    inverse = lax.rsqrt(variance + norm_eps)
    return centered * inverse, inverse


def norm_grad(vhat, inverse, e_hat):
    mean_e = jnp.mean(e_hat, axis=-1, keepdims=True)
    mean_ev = jnp.mean(e_hat * vhat, axis=-1, keepdims=True)
    return inverse * (e_hat - mean_e - vhat * mean_ev)


def block_kernel(
    n_bits,
    tok_in, cot_in, mask_in, step_in, table_in, w_ada_in, b_ada_in, gain_one_in, wqkv_in, wout_in, gain_two_in,
    wup_in, bup_in, wdown_in, b_down_in, cos_in, sin_in,
    mixed_out, grad_tok_out, gathered_out, grads_out,
    tok, cot, gb, n2, normed, wqkv, wout, wup, wdown, proj, ho, do, lse, attn, mid, part, hidden, gel,
    grad_mid, send_a, recv_a, recv_b, recv_c, acc, oth, stage,
    mod, vec, bup, ada_line, lines, mask_line, cos_t, sin_t, sums, sums_recv, sums_low,
    ssem, rsem, lsem, *stage_recv,
):
    wide = lax.axis_index("wide")
    narrow = lax.axis_index("narrow")
    core = lax.rem(narrow, 2)
    chip_y = lax.div(narrow, 2)
    sib = (wide, narrow + 1 - 2 * core)
    across = (wide, lax.rem(narrow + 2, 4))

    def wide_bit(level):
        return lax.rem(lax.div(wide, 1 << level), 2)

    def wide_peer(level):
        return (wide + (1 << level) * (1 - 2 * wide_bit(level)), narrow)

    peers = [sib, across] + [wide_peer(level) for level in range(n_bits)]
    own0 = core * ROWS_LOCAL
    sib0 = (1 - core) * ROWS_LOCAL

    n_sems = {"remote": 0, "local": 0}

    def remote(src, dst, peer):
        at = n_sems["remote"]
        n_sems["remote"] += 1
        return pltpu.make_async_remote_copy(
            src_ref=src, dst_ref=dst, send_sem=ssem.at[at], recv_sem=rsem.at[at],
            device_id=peer, device_id_type=MESH,
        )

    def local(src, dst):
        at = n_sems["local"]
        n_sems["local"] += 1
        return pltpu.make_async_copy(src, dst, lsem.at[at])

    c_tok = local(tok_in, tok)
    c_cot = local(cot_in, cot)
    c_small = [
        local(b_ada_in, ada_line),
        local(gain_one_in, lines[0]),
        local(gain_two_in, lines[1]),
        local(b_down_in, lines[2]),
        local(bup_in, bup[0]),
        local(mask_in, mask_line),
        local(cos_in, cos_t),
        local(sin_in, sin_t),
    ]
    c_wqkv = local(wqkv_in, wqkv.at[0])
    c_wout = local(wout_in, wout.at[pl.ds(0, 192)])
    c_wup = local(wup_in, wup.at[:, pl.ds(0, D)])
    c_wdown = local(wdown_in, wdown.at[pl.ds(0, D)])
    c_tok.start()
    for copy in c_small:
        copy.start()
    c_wqkv.start()
    c_cot.start()
    c_wout.start()
    c_wup.start()
    c_wdown.start()

    barrier = pltpu.get_barrier_semaphore()
    for peer in peers:
        pl.semaphore_signal(barrier, inc=1, device_id=peer, device_id_type=MESH)
    pl.semaphore_wait(barrier, len(peers))

    r_tok = remote(tok_in, n2.at[rows_at(own0, ROWS_LOCAL, 512)], sib)
    r_cot = remote(cot, gb.at[rows_at(own0, ROWS_LOCAL, 512)], sib)
    r_tok.start()

    places = {
        "q": (wqkv_in, lambda rows: wqkv.at[1, rows], QKV_ROWS, 0),
        "o": (wout_in, lambda rows: wout.at[rows], 192, 192),
        "u": (wup_in, lambda rows: wup.at[rows, pl.ds(D, D)], D, 0),
        "d": (wdown_in, lambda rows: wdown.at[rows], D, D),
    }
    w_across, w_along, plans = {}, {}, {}
    piece_keys = []
    for matrix in PIECES:
        source, target, total_rows, shift = places[matrix]
        count = len(PIECES[matrix])
        size = total_rows // (2 * count)
        for piece in range(count):
            level = PIECES[matrix][piece]
            row = 2 * size * piece + wide_bit(level) * size
            here = target(rows_at(shift + row, size, 16))
            key = "W" + matrix + str(piece)
            piece_keys.append(key)
            w_across[key] = remote(source.at[rows_at(row, size, 16)], here, across)
            w_along[key] = remote(here, here, wide_peer(level))
    ahead = 6

    def forward_piece(at):
        w_across[piece_keys[at]].wait_recv()
        w_along[piece_keys[at]].start()
        if at + ahead < len(piece_keys):
            w_across[piece_keys[at + ahead]].start()

    for at, key in enumerate(piece_keys):
        plans[key] = [functools.partial(forward_piece, at)]
    r_bup = remote(bup_in, bup[1], across)
    for key in piece_keys[:ahead]:
        w_across[key].start()
    r_bup.start()

    def segment(name, index):
        offset, rows = CHUNKS[name]
        for dim, halved, count, _ in chunk_stages(name, n_bits)[:index]:
            if halved:
                offset = offset + wide_bit(dim) * count
                rows = count
        return offset, rows

    stage_copies, back_copies, stage_base, returns, final_copies, outbox = {}, {}, {}, {}, {}, {}
    stage_rows_used = 0
    n_stages = n_bits + 1
    for index in range(n_stages):
        base = 0
        for name in CHUNKS:
            dim, halved, count, both = chunk_stages(name, n_bits)[index]
            offset, _ = segment(name, index)
            stage_base[name, index] = base
            if dim == "y":
                sent, peer = [oth], across
            else:
                sent, peer = [acc, oth] if both else [acc], wide_peer(dim)
                if halved:
                    offset = offset + (1 - wide_bit(dim)) * count
            copies = []
            for array in sent:
                landing = stage_recv[index].at[pl.ds(base, count)]
                source = array.at[rows_at(offset, count, 16)]
                if halved and array is acc:
                    if both:
                        outbox[name, index] = (stage, stage_rows_used)
                        source = stage.at[pl.ds(stage_rows_used, count)]
                        stage_rows_used += count
                    else:
                        outbox[name, index] = (oth, offset)
                        source = oth.at[rows_at(offset, count, 16)]
                copies.append(remote(source, landing, peer))
                base += count
            stage_copies[name, index] = copies
            if halved:
                offset, count = segment(name, index + 1)
                rows = acc.at[rows_at(offset, count, 16)]
                back_copies[name, index] = remote(rows, rows, peer)
    for name in CHUNKS:
        returns[name] = [at for at in range(n_stages) if (name, at) in back_copies]
        first, count = CHUNKS[name]
        final_copies[name] = local(acc.at[pl.ds(first, count)], grads_out.at[pl.ds(first, count)])

    def start_stage(name, index):
        if index == 0 and (name, 0) in outbox:
            offset, _ = segment(name, 0)
            dim, _, count, _ = chunk_stages(name, n_bits)[0]
            box, row0 = outbox[name, 0]
            box[pl.ds(row0, count), :] = acc[rows_at(offset + (1 - wide_bit(dim)) * count, count, 16), :]
        for copy in stage_copies[name, index]:
            copy.start()

    def merge_step(name, index):
        for copy in stage_copies[name, index - 1]:
            copy.wait()
        offset, rows = segment(name, index)
        both_before = len(stage_copies[name, index - 1]) == 2
        base = stage_base[name, index - 1]
        brought = stage_recv[index - 1]

        def merge(array, row0, count, box=None):
            start = base + rows if array is oth else base
            step = 48 if count % 48 == 0 else 16
            target, target0 = box or (array, row0)

            def one(at):
                row = row0 + step * at
                here = rows_at(row, step, 16)
                value = array[here, :].astype(f32) + brought[rows_at(start + row - offset, step, 16), :].astype(f32)
                target[rows_at(target0 + step * at, step, 16), :] = value.astype(bf16)

            loop(count // step, one)

        arrays = [acc, oth] if both_before else [acc]
        if index == n_stages:
            merge(acc, offset, rows)
            back_copies[name, returns[name][-1]].start()
            return
        dim, halved, count, _ = chunk_stages(name, n_bits)[index]
        if dim == "y":
            for array in reversed(arrays):
                merge(array, offset, rows)
                if array is oth or not both_before:
                    start_stage(name, index)
        elif halved:
            for array in arrays:
                box = outbox[name, index] if array is acc else None
                merge(array, offset + (1 - wide_bit(dim)) * count, count, box)
            start_stage(name, index)
            for array in arrays:
                merge(array, offset + wide_bit(dim) * count, count)
        else:
            merge(acc, offset, rows)
            start_stage(name, index)

    def back_step(name, at):
        back_copies[name, returns[name][at]].wait()
        if at > 0:
            back_copies[name, returns[name][at - 1]].start()
        else:
            final_copies[name].start()

    for name in CHUNKS:
        plan = [functools.partial(start_stage, name, 0)]
        plan += [functools.partial(merge_step, name, index + 1) for index in range(n_stages)]
        plan += [functools.partial(back_step, name, at) for at in reversed(range(len(returns[name])))]
        plans[name] = plan

    place = 2 * wide + chip_y
    r_sib, row_copies, own_rows = [], [], []
    for part_index in range(2):
        mine = gathered_out.at[part_index, core]
        r_sib.append(remote(sums.at[part_index], sums_recv.at[part_index], sib))
        own_rows.append(local(sums_low.at[part_index], mine.at[place]))
        copies = [remote(sums_low.at[part_index], mine.at[place], across)]
        for level in range(n_bits):
            count = 2 << level
            rows = mine.at[pl.ds(lax.div(place, count) * count, count)]
            copies.append(remote(rows, rows, wide_peer(level)))
        copies.append(remote(mine, mine, sib))
        row_copies.append(copies)

    def row_step(part_index, at):
        if at == 0:
            own_rows[part_index].start()
        if at == 1:
            own_rows[part_index].wait()
        if at > 0:
            row_copies[part_index][at - 1].wait()
        if at < n_bits + 2:
            row_copies[part_index][at].start()

    for part_index, key in enumerate(("re", "rl")):
        plans[key] = [functools.partial(row_step, part_index, at) for at in range(n_bits + 3)]

    def sums_ready(part_index):
        r_sib[part_index].wait()
        cols = rows_at(core * 384, 384, 128)
        total = sums[part_index, :, cols] + sums_recv[part_index, :, cols]
        sums_low[part_index] = total.astype(bf16)

    steps_at = {}
    for name in PLACES:
        if name[0] == "w":
            keys = [key for key in piece_keys if key[1] == name[1]]
            steps_at[name] = [step for key in keys for step in plans.pop(key)]
        else:
            steps_at[name] = [plans[key].pop(0) for key in SCHEDULE.get(name, ()) if plans.get(key)]
    while any(plans.values()):
        steps_at["g3"] += [plans[key].pop(0) for key in plans if plans[key]]

    def point(name):
        for step in steps_at[name]:
            step()

    def need(matrix):
        point("w" + matrix)
        for key in piece_keys:
            if key[1] == matrix:
                w_along[key].wait_recv()

    for copy in c_small:
        copy.wait()
    time_step = step_in[chip_y]
    for row in range(3):
        vec[row : row + 1, :] = lines[row][...].reshape(1, D)

    def modulation(table, w_ada):
        copies = [local(table_in, table), local(w_ada_in, w_ada)]
        for copy in copies:
            copy.start()
        for copy in copies:
            copy.wait()
        picked = table[pl.ds(time_step, 1), :]
        cond = picked / (1.0 + jnp.exp(-picked))
        cond = jnp.broadcast_to(cond, (16, 128)).astype(bf16)
        for index in range(6):
            flat = dot(cond, w_ada[:, index * D : (index + 1) * D], NN)
            mod[index : index + 1, :] = ada_line[pl.ds(index * D, D)].reshape(1, D) + flat[0:1, :]

    pl.run_scoped(modulation, pltpu.VMEM((1000, 128), f32), pltpu.VMEM((128, 6 * D), bf16))

    def first_norm(source, src0, dst0):
        def one(index):
            values = source[rows_at(src0 + 128 * index, 128, 128), :].astype(f32)
            vhat, _ = normalize(values)
            out = vhat * vec[0:1, :] * (1.0 + mod[1:2, :]) + mod[0:1, :]
            normed[rows_at(dst0 + 128 * index, 128, 128), :] = out.astype(bf16)

        loop(4, one)

    c_tok.wait()
    first_norm(tok, 0, own0)
    point("n0")
    r_tok.wait_recv()
    first_norm(n2, sib0, sib0)
    c_cot.wait()
    mask = jnp.broadcast_to(mask_line[...].astype(f32).reshape(1, ROWS_LOCAL), (8, ROWS_LOCAL)).T[:, 0:1]
    cot[...] = (cot[...].astype(f32) * mask).astype(bf16)
    r_cot.start()
    point("n1")

    def project(shard):
        def one(index):
            cols = rows_at(256 * index, 256, 256)
            flat = dot(wqkv[shard], normed[cols, :], NT)
            cos_b, sin_b = cos_t[:, cols], sin_t[:, cols]
            for kind in (0, 1):
                scale = 0.125 if kind == 0 else 1.0
                for head in range(SHARD_HEADS):
                    at = kind * 192 + head * HD
                    low, high = flat[at : at + 32], flat[at + 32 : at + 64]
                    proj[shard, at : at + 32, cols] = ((low * cos_b - high * sin_b) * scale).astype(bf16)
                    proj[shard, at + 32 : at + 64, cols] = ((high * cos_b + low * sin_b) * scale).astype(bf16)
            proj[shard, 384:576, cols] = flat[384:576].astype(bf16)
            point_in("p", 2 * shard + lax.div(index, 2), lax.rem(index, 2) == 1, 4)

        loop(4, one)

    def point_in(prefix, index, last, count):
        for place in range(count):
            if steps_at.get(prefix + str(place)) and (prefix, place) != ("u", 3):

                @pl.when((index == place) & last)
                def _():
                    point(prefix + str(place))

    def head_rows(kind, head):
        return rows_at(kind * 192 + head * HD, HD, HD)

    def attend(shard, head):
        q_t = proj[shard, head_rows(0, head), :]
        k_t = proj[shard, head_rows(1, head), :]
        v_t = proj[shard, head_rows(2, head), :]
        scores = dot(k_t, q_t, TN)
        top = jnp.max(scores, axis=0, keepdims=True)
        weights = jnp.exp(scores - top)
        total = jnp.sum(weights, axis=0, keepdims=True)
        out = dot(v_t, weights.astype(bf16), NN) * (1.0 / total)
        index = shard * SHARD_HEADS + head
        ho[rows_at(index * HD, HD, HD), :] = out.astype(bf16)
        lse[index, 0:1, :] = top + jnp.log(total)

    c_wqkv.wait()

    def shard_heads(shard):
        @pl.when(shard == 1)
        def _():
            need("q")

        project(shard)

        def one(head):
            attend(shard, head)
            point_in("a", SHARD_HEADS * shard + head, True, 6)

        loop(SHARD_HEADS, one)

    loop(2, shard_heads)

    c_wout.wait()
    need("o")
    half = 256

    def exchange_start(recv, index):
        rows = pl.ds(half * index, half)
        copy = remote(send_a.at[rows], recv.at[rows], sib)
        copy.start()
        return copy

    r_attn = []
    for index in range(2):
        out = dot(ho[:, rows_at(sib0 + half * index, half, half)], wout[...], TN)
        send_a[half * index : half * (index + 1), :] = out.astype(bf16)
        r_attn.append(exchange_start(recv_a, index))
    for index in range(2):
        out = dot(ho[:, rows_at(own0 + half * index, half, half)], wout[...], TN)
        attn[half * index : half * (index + 1), :] = out
    point("o0")
    r_n2 = []
    for index in range(2):
        r_attn[index].wait_recv()

        def second_norm(sub):
            rows = rows_at(half * index + 128 * sub, 128, 128)
            value = attn[rows, :] + recv_a[rows, :].astype(f32)
            attn[rows, :] = value
            residual = tok[rows, :].astype(f32) + mod[2:3, :] * value
            mid[rows, :] = residual
            vhat, _ = normalize(residual)
            out = vhat * vec[1:2, :] * (1.0 + mod[4:5, :]) + mod[3:4, :]
            n2[rows_at(own0 + half * index + 128 * sub, 128, 128), :] = out.astype(bf16)

        loop(2, second_norm)
        rows = rows_at(own0 + half * index, half, half)
        r_n2.append(remote(n2.at[rows], n2.at[rows], sib))
        r_n2[index].start()
        r_attn[index].wait_send()

    r_cot.wait_recv()

    def branch_grad(index):
        rows = rows_at(own0 + 128 * index, 128, 128)
        part_rows = rows_at(128 * index, 128, 128)
        gb[rows, :] = (cot[part_rows, :].astype(f32) * mod[5:6, :]).astype(bf16)
        rows = rows_at(sib0 + 128 * index, 128, 128)
        gb[rows, :] = (gb[rows, :].astype(f32) * mod[5:6, :]).astype(bf16)

    r_cot.wait_send()
    loop(4, branch_grad)
    point("o1")

    c_wup.wait()
    r_bup.wait_recv()
    for row in range(2):
        vec[4 + row : 5 + row, :] = bup[row][...].reshape(1, D)
    gelu_c = math.sqrt(2.0 / math.pi)

    def up(index):
        shard = lax.div(index, 4)
        block = lax.rem(index, 4)

        @pl.when(index == 2)
        def _():
            r_n2[0].wait_recv()
            r_n2[1].wait_recv()

        @pl.when(index == 4)
        def _():
            point("u3")
            need("u")

        rows = rows_at(lax.rem(own0 + 256 * block, LEN), 256, 256)
        cols = rows_at(shard * D, D, D)
        pre = dot(n2[rows, :], wup[:, cols], NN) + vec[pl.ds(4 + shard, 1), :]
        square = pre * pre
        squash = jnp.tanh(gelu_c * pre * (1.0 + 0.044715 * square))
        gate = 0.5 * (1.0 + squash)
        hidden[rows, cols] = (pre * gate).astype(bf16)
        slope = gate + 0.5 * pre * (1.0 - squash * squash) * (gelu_c * (1.0 + 3.0 * 0.044715 * square))
        gel[rows, cols] = slope.astype(bf16)

        point_in("u", index, True, 8)

    loop(8, up)

    def w_down_grad(shard, target, base):
        def one(index):
            cols = rows_at(shard * D + 256 * index, 256, 256)
            out = dot(hidden[:, cols], gb[...], TN)
            target[rows_at(base + 256 * index, 256, 256), :] = out.astype(bf16)

        loop(3, one)

    w_down_grad(1, oth, 0)
    point("f0")
    w_down_grad(0, acc, 0)
    point("f1")

    sums[...] = jnp.zeros_like(sums)
    c_wdown.wait()

    def hidden_grad(shard, row):
        def one(index):
            rows = rows_at(256 * index, 256, 256)
            cols = pl.ds(shard * D, D)
            grad_act = dot(gb[rows, :], wdown[pl.ds(shard * D, D), :], NT)
            low = (grad_act * gel[rows, cols].astype(f32)).astype(bf16)
            gel[rows, cols] = low
            line = pl.ds(row, 1)
            sums[1, line, :] = sums[1, line, :] + jnp.sum(low.astype(f32), axis=0, keepdims=True)

        loop(4, one)

    def w_up_grad(shard, target):
        def one(index):
            cols = rows_at(256 * index, 256, 256)
            out = dot(n2[:, cols], gel[:, pl.ds(shard * D, D)], TN)
            target[rows_at(D + 256 * index, 256, 256), :] = out.astype(bf16)

        loop(3, one)

    hidden_grad(0, 3 + narrow)
    point("f2")
    need("d")
    hidden_grad(1, 3 + lax.rem(narrow + 2, 4))
    point("f3")
    w_up_grad(1, oth)
    point("f4")
    w_up_grad(0, acc)
    point("f5")

    r_gn2 = []
    for index in range(2):
        out = dot(gel[rows_at(sib0 + half * index, half, half), :], wup[...], NT)
        send_a[half * index : half * (index + 1), :] = out.astype(bf16)
        r_gn2.append(exchange_start(recv_b, index))
    for index in range(2):
        out = dot(gel[rows_at(own0 + half * index, half, half), :], wup[...], NT)
        part[half * index : half * (index + 1), :] = out
    point("f6")

    r_ga = []
    for index in range(2):
        r_gn2[index].wait()

        def second_back(sub):
            rows = rows_at(half * index + 128 * sub, 128, 128)
            upstream = part[rows, :] + recv_b[rows, :].astype(f32)
            vhat, inverse = normalize(mid[rows, :])
            scaled = upstream * (1.0 + mod[4:5, :])
            grad_mixed = cot[rows, :].astype(f32)
            value = grad_mixed + norm_grad(vhat, inverse, scaled * vec[1:2, :])
            grad_mid[rows, :] = value
            gb[rows_at(own0 + half * index + 128 * sub, 128, 128), :] = (value * mod[2:3, :]).astype(bf16)
            add_sum(0, 0, value * attn[rows, :])
            add_sum(0, 1, upstream)
            add_sum(0, 2, upstream * (vhat * vec[1:2, :]))
            add_sum(0, 4, scaled * vhat)
            add_sum(0, 5, grad_mixed * mod[5:6, :])

        def add_sum(part_index, row, values):
            line = slice(row, row + 1)
            sums[part_index, line, :] = sums[part_index, line, :] + jnp.sum(values, axis=0, keepdims=True)

        loop(2, second_back)
        rows = rows_at(own0 + half * index, half, half)
        r_ga.append(remote(gb.at[rows], gb.at[rows], sib))
        r_ga[index].start()
    point("f7")

    r_branch = []
    for index in range(2):
        out = dot(hidden[rows_at(sib0 + half * index, half, half), :], wdown[...], NN)
        send_a[half * index : half * (index + 1), :] = out.astype(bf16)
        r_branch.append(exchange_start(recv_c, index))
    for index in range(2):
        out = dot(hidden[rows_at(own0 + half * index, half, half), :], wdown[...], NN)
        part[half * index : half * (index + 1), :] = out
    point("f8")

    r_ga[0].wait_recv()
    r_ga[1].wait_recv()

    def head_grad(index):
        cols = rows_at(256 * index, 256, 256)
        do[:, cols] = dot(wout[...], gb[cols, :], NT).astype(bf16)

    loop(4, head_grad)
    point("h0")
    oth[1536:1728, :] = dot(ho[192:384, :], gb[...], NN).astype(bf16)
    acc[1536:1728, :] = dot(ho[0:192, :], gb[...], NN).astype(bf16)
    point("h1")

    def finish_branch(index):
        rows = rows_at(128 * index, 128, 128)
        branch = part[rows, :] + recv_c[rows, :].astype(f32) + vec[2:3, :]
        add_sum(0, 3, cot[rows, :].astype(f32) * branch)
        send_a[rows, :] = (mid[rows, :] + mod[5:6, :] * branch).astype(bf16)

    r_branch[0].wait()
    r_branch[1].wait()
    loop(4, finish_branch)
    c_mixed = local(send_a, mixed_out)
    c_mixed.start()
    on_first = (1 - core).astype(f32)
    high = lax.div(time_step, 32)
    sums[0, 6:7, :] = jnp.full((1, D), high.astype(f32) * on_first)
    sums[0, 7:8, :] = jnp.full((1, D), (time_step - 32 * high).astype(f32) * on_first)
    r_sib[0].start()
    point("h2")

    def attend_back(shard, head):
        q_t = proj[shard, head_rows(0, head), :]
        k_t = proj[shard, head_rows(1, head), :]
        v_t = proj[shard, head_rows(2, head), :]
        index = shard * SHARD_HEADS + head
        d_t = do[rows_at(index * HD, HD, HD), :]
        probs = jnp.exp(dot(k_t, q_t, TN) - lse[index, 0:1, :])
        grad_probs = dot(v_t, d_t, TN)
        inner = jnp.sum(probs * grad_probs, axis=0, keepdims=True)
        grad_scores = (probs * (grad_probs - inner)).astype(bf16)
        dq_t = dot(k_t, grad_scores, NN) * 0.125
        dk_t = dot(grad_scores, q_t, NT).T
        dv_t = dot(probs.astype(bf16), d_t, NT).T
        for kind, grad in ((0, dq_t), (1, dk_t)):
            low, high = grad[:32], grad[32:]
            turned = jnp.concatenate(
                [low * cos_t[...] + high * sin_t[...], high * cos_t[...] - low * sin_t[...]], axis=0
            )
            proj[shard, head_rows(kind, head), :] = turned.astype(bf16)
        proj[shard, head_rows(2, head), :] = dv_t.astype(bf16)

    for key in piece_keys:
        w_along[key].wait_send()
        w_across[key].wait_send()

    def w_qkv_grad(shard, target):
        def one(index):
            rows = rows_at(192 * index, 192, 64)
            out = dot(proj[shard, rows, :], normed[...], NN)
            target[rows_at(1728 + 192 * index, 192, 64), :] = out.astype(bf16)

        loop(3, one)

    def back_heads(index):
        shard = 1 - lax.div(index, SHARD_HEADS)
        head = lax.rem(index, SHARD_HEADS)
        attend_back(shard, head)

        @pl.when(index == 0)
        def _():
            sums_ready(0)

        point_in("b", index, True, 6)

        @pl.when(index == 2)
        def _():
            w_qkv_grad(1, oth)
            point("bx")

    loop(6, back_heads)
    w_qkv_grad(0, acc)
    point("by")

    def normed_grad(offset):
        first = dot(proj[0, :, offset], wqkv[0], TN)
        return first + dot(proj[1, :, offset], wqkv[1], TN)

    c_mixed.wait()
    r_gn = []
    for index in range(2):
        send_a[half * index : half * (index + 1), :] = normed_grad(
            rows_at(sib0 + half * index, half, half)
        ).astype(bf16)
        r_gn.append(exchange_start(recv_a, index))
    for index in range(2):
        part[half * index : half * (index + 1), :] = normed_grad(rows_at(own0 + half * index, half, half))
    point("g0")
    for index in range(2):
        r_gn[index].wait()

        def first_back(sub):
            rows = rows_at(half * index + 128 * sub, 128, 128)
            upstream = part[rows, :] + recv_a[rows, :].astype(f32)
            vhat, inverse = normalize(tok[rows, :].astype(f32))
            scaled = upstream * (1.0 + mod[1:2, :])
            part[rows, :] = grad_mid[rows, :] + norm_grad(vhat, inverse, scaled * vec[0:1, :])
            add_sum(1, 0, upstream)
            add_sum(1, 1, upstream * (vhat * vec[0:1, :]))
            add_sum(1, 2, scaled * vhat)

        loop(2, first_back)
    c_grad_tok = local(part, grad_tok_out)
    c_grad_tok.start()

    r_sib[1].start()
    point("g1")
    sums_ready(1)
    point("g2")
    point("g3")
    for name in CHUNKS:
        final_copies[name].wait()
    c_grad_tok.wait()
    for copy in [r_tok, r_bup] + r_n2 + r_ga:
        copy.wait_send()


def fused_block(n_wide, tokens, cot, mask, timestep, table, w_ada, b_ada, gain_one, w_qkv_t, w_out, gain_two, w_up, b_up,
                w_down, b_down, cos_t, sin_t):
    n_bits = n_wide.bit_length() - 1
    any_space = pl.BlockSpec(memory_space=pl.ANY)
    scratch = [
        pltpu.VMEM((ROWS_LOCAL, D), bf16),
        pltpu.VMEM((ROWS_LOCAL, D), bf16),
        pltpu.VMEM((LEN, D), bf16),
        pltpu.VMEM((LEN, D), bf16),
        pltpu.VMEM((LEN, D), bf16),
        pltpu.VMEM((2, QKV_ROWS, D), bf16),
        pltpu.VMEM((384, D), bf16),
        pltpu.VMEM((D, 2 * D), bf16),
        pltpu.VMEM((2 * D, D), bf16),
        pltpu.VMEM((2, QKV_ROWS, LEN), bf16),
        pltpu.VMEM((384, LEN), bf16),
        pltpu.VMEM((384, LEN), bf16),
        pltpu.VMEM((6, 8, LEN), f32),
        pltpu.VMEM((ROWS_LOCAL, D), f32),
        pltpu.VMEM((ROWS_LOCAL, D), f32),
        pltpu.VMEM((ROWS_LOCAL, D), f32),
        pltpu.VMEM((LEN, 2 * D), bf16),
        pltpu.VMEM((LEN, 2 * D), bf16),
        pltpu.VMEM((ROWS_LOCAL, D), f32),
        pltpu.VMEM((ROWS_LOCAL, D), bf16),
        pltpu.VMEM((ROWS_LOCAL, D), bf16),
        pltpu.VMEM((ROWS_LOCAL, D), bf16),
        pltpu.VMEM((ROWS_LOCAL, D), bf16),
        pltpu.VMEM((GRAD_ROWS, D), bf16),
        pltpu.VMEM((GRAD_ROWS, D), bf16),
        pltpu.VMEM((outbox_rows(n_bits), D), bf16),
        pltpu.VMEM((8, D), f32),
        pltpu.VMEM((8, D), f32),
        [pltpu.VMEM((D,), f32)] * 2,
        pltpu.VMEM((6 * D,), f32),
        [pltpu.VMEM((D,), f32)] * 3,
        pltpu.VMEM((ROWS_LOCAL,), jnp.int32),
        pltpu.VMEM((32, LEN), f32),
        pltpu.VMEM((32, LEN), f32),
        pltpu.VMEM((2, 8, D), f32),
        pltpu.VMEM((2, 8, D), f32),
        pltpu.VMEM((2, 8, D // 2), bf16),
        pltpu.SemaphoreType.DMA((240,)),
        pltpu.SemaphoreType.DMA((240,)),
        pltpu.SemaphoreType.DMA((48,)),
    ]
    for index in range(n_bits + 1):
        scratch.append(pltpu.VMEM((stage_rows(index, n_bits), D), bf16))
    specs = [any_space] * 17
    specs[3] = pl.BlockSpec(memory_space=pltpu.SMEM)
    return pl.pallas_call(
        functools.partial(block_kernel, n_bits),
        out_shape=(
            jax.ShapeDtypeStruct((ROWS_LOCAL, D), bf16),
            jax.ShapeDtypeStruct((ROWS_LOCAL, D), f32),
            jax.ShapeDtypeStruct((2, 2, 2 * n_wide, 8, D // 2), bf16),
            jax.ShapeDtypeStruct((GRAD_ROWS, D), bf16),
        ),
        in_specs=specs,
        out_specs=[any_space] * 4,
        scratch_shapes=scratch,
        compiler_params=pltpu.CompilerParams(
            collective_id=0, has_side_effects=True, vmem_limit_bytes=60 * 1024 * 1024
        ),
    )(tokens, cot, mask, timestep, table, w_ada, b_ada, gain_one, w_qkv_t, w_out, gain_two, w_up, b_up, w_down, b_down,
      cos_t, sin_t)


def finish_kernel(
    gathered_in, table_in, w_ada_in, grads_in, mixed_in, grad_tok_in,
    mixed_out, grad_tok_out, g_table, g_w_ada, g_b_ada, g_gain_one, g_wqkv, g_wout, g_gain_two, g_wup, g_bup,
    g_wdown, g_b_down,
    gathered, table, w_ada, grads, mod_low, table_out, ada_out, wide_out, late_sum, mixed_buf, tok_buf, lines, sem,
):
    pieces = GRAD_ROWS // 192
    targets = [(g_wdown, 0), (g_wup, 768), (g_wout, 1536), (g_wqkv, 1728)]
    loads = [(gathered_in, gathered), (table_in, table), (w_ada_in, w_ada)]
    loads = [pltpu.make_async_copy(src, dst, sem.at[at]) for at, (src, dst) in enumerate(loads)]
    pass_in = [
        pltpu.make_async_copy(mixed_in, mixed_buf, sem.at[3]),
        pltpu.make_async_copy(grad_tok_in, tok_buf, sem.at[4]),
    ]
    pass_out = [
        pltpu.make_async_copy(mixed_buf, mixed_out, sem.at[5]),
        pltpu.make_async_copy(tok_buf, grad_tok_out, sem.at[6]),
    ]
    grad_in, grad_out = [], []
    for piece in range(pieces):
        rows = pl.ds(192 * piece, 192)
        grad_in.append(pltpu.make_async_copy(grads_in.at[rows], grads.at[rows], sem.at[7 + piece]))
        target, first = [item for item in targets if item[1] <= 192 * piece][-1]
        grad_out.append(
            pltpu.make_async_copy(
                wide_out.at[rows], target.at[pl.ds(192 * piece - first, 192)], sem.at[7 + pieces + piece]
            )
        )
    for copy in loads + pass_in + grad_in:
        copy.start()
    for copy in loads:
        copy.wait()

    def both(index):
        return jnp.concatenate([gathered[index, 0].astype(f32), gathered[index, 1].astype(f32)], axis=-1)

    early, late = both(0), both(1)
    total_early, total_late = jnp.sum(early, axis=0), jnp.sum(late, axis=0)
    late_sum[...] = total_late
    for row, values in enumerate([late[:, 0], late[:, 1], early[:, 0], early[:, 1], early[:, 2], early[:, 3]]):
        mod_low[:, row * D : (row + 1) * D] = values.astype(bf16)
    rows = [total_late[0:1], total_late[1:2]] + [total_early[row : row + 1] for row in range(4)]
    for row, values in enumerate(rows):
        lines[0][pl.ds(row * D, D)] = values.reshape(D)
    lines[1][...] = total_late[2:3].reshape(D)
    lines[2][...] = total_early[4:5].reshape(D)
    lines[3][...] = late_sum[pl.ds(3 + lax.axis_index("narrow"), 1), :].reshape(D)
    lines[4][...] = total_early[5:6].reshape(D)
    line_out = [
        pltpu.make_async_copy(line, out, sem.at[7 + 2 * pieces + at])
        for at, (line, out) in enumerate(zip(lines, (g_b_ada, g_gain_one, g_gain_two, g_bup, g_b_down)))
    ]
    for copy in line_out:
        copy.start()
    seqs, steps = early.shape[0], table.shape[0]
    time_step = early[:, 6, 0:1] * 32.0 + early[:, 7, 0:1]
    columns = lax.broadcasted_iota(jnp.int32, (seqs, steps), 1).astype(f32)
    pick = jnp.where(columns == time_step, 1.0, 0.0).astype(f32)
    picked = lax.dot_general(pick, table[...], NN, precision=highest, preferred_element_type=f32)
    gate = 1.0 / (1.0 + jnp.exp(-picked))
    cond = (picked * gate).astype(bf16)
    ada_out[...] = dot(cond, mod_low[...], TN)
    out_ada = pltpu.make_async_copy(ada_out, g_w_ada, sem.at[7 + 2 * pieces + 5])
    out_ada.start()
    grad_cond = dot(mod_low[...], w_ada[...], NT) * (gate * (1.0 + picked * (1.0 - gate)))
    table_out[...] = lax.dot_general(pick, grad_cond, TN, precision=highest, preferred_element_type=f32)
    out_table = pltpu.make_async_copy(table_out, g_table, sem.at[7 + 2 * pieces + 6])
    out_table.start()
    for at in range(2):
        pass_in[at].wait()
        pass_out[at].start()
    for piece in range(pieces):
        grad_in[piece].wait()
        rows = pl.ds(192 * piece, 192)
        wide_out[rows, :] = grads[rows, :].astype(f32)
        grad_out[piece].start()
    for copy in line_out + [out_ada, out_table] + pass_out + grad_out:
        copy.wait()


def finish(gathered, table, w_ada, grads, mixed, grad_tokens):
    seqs, steps = gathered.shape[2], table.shape[0]
    any_space = pl.BlockSpec(memory_space=pl.ANY)
    shapes = [
        (mixed.shape, bf16), (grad_tokens.shape, f32), (table.shape, f32), (w_ada.shape, f32), ((6 * D,), f32),
        ((D,), f32), ((QKV_ROWS, D), f32), ((192, D), f32), ((D,), f32), ((D, D), f32), ((D,), f32), ((D, D), f32),
        ((D,), f32),
    ]
    return pl.pallas_call(
        finish_kernel,
        out_shape=tuple(jax.ShapeDtypeStruct(shape, kind) for shape, kind in shapes),
        in_specs=[any_space] * 6,
        out_specs=[any_space] * len(shapes),
        scratch_shapes=[
            pltpu.VMEM(gathered.shape, bf16),
            pltpu.VMEM(table.shape, f32),
            pltpu.VMEM(w_ada.shape, bf16),
            pltpu.VMEM(grads.shape, bf16),
            pltpu.VMEM((seqs, 6 * D), bf16),
            pltpu.VMEM((steps, table.shape[1]), f32),
            pltpu.VMEM(w_ada.shape, f32),
            pltpu.VMEM(grads.shape, f32),
            pltpu.VMEM((8, D), f32),
            pltpu.VMEM(mixed.shape, bf16),
            pltpu.VMEM(grad_tokens.shape, f32),
            [pltpu.VMEM((6 * D,), f32)] + [pltpu.VMEM((D,), f32)] * 4,
            pltpu.SemaphoreType.DMA((48,)),
        ],
        compiler_params=pltpu.CompilerParams(vmem_limit_bytes=56 * 1024 * 1024),
    )(gathered, table, w_ada, grads, mixed, grad_tokens)


def rope_tables():
    half_width = HD // 2
    frequency = np.float32(10000.0) ** (np.float32(-2.0) * np.arange(half_width, dtype=np.float32) / np.float32(HD))
    angles = np.arange(LEN, dtype=np.float32)[None, :] * frequency[:, None]
    return np.cos(angles).astype(np.float32), np.sin(angles).astype(np.float32)


def body(tokens, timestep, token_mask, time_table, w_ada, b_ada, gain_one, w_qkv, w_out, gain_two, w_up, b_up,
         w_down, b_down, cotangent):
    n_wide = lax.axis_size("wide")
    cos_t, sin_t = rope_tables()
    w_qkv_t = jnp.transpose(w_qkv, (0, 2, 1)).reshape(QKV_ROWS, D)
    mixed, grad_tokens, gathered, grads = fused_block(
        n_wide, tokens, cotangent, token_mask, timestep, time_table, w_ada, b_ada, gain_one, w_qkv_t, w_out, gain_two,
        w_up, b_up, w_down, b_down, cos_t, sin_t,
    )
    outs = list(finish(gathered, time_table, w_ada, grads, mixed, grad_tokens))
    outs[6] = jnp.transpose(outs[6].reshape(3, 192, D), (0, 2, 1))
    return tuple(outs)


def solution(mesh):
    return jax.shard_map(
        body,
        mesh=mesh,
        in_specs=(
            P(("wide", "narrow"), None), P("wide"), P(("wide", "narrow")), P(), P(), P(), P(),
            P(None, None, "narrow"), P("narrow", None), P(), P(None, "narrow"), P("narrow"), P("narrow", None), P(),
            P(("wide", "narrow"), None),
        ),
        out_specs=(
            P(("wide", "narrow"), None), P(("wide", "narrow"), None), P(), P(), P(), P(), P(None, None, "narrow"),
            P("narrow", None), P(), P(None, "narrow"), P("narrow"), P("narrow", None), P(),
        ),
        check_vma=False,
    )
```

time: 836 us -> 155 us (0.19)
  waiting for transfers between devices: 352 us -> 0 us
  matrix products: 232 us -> 0 us
  Pallas kernels: 0 us -> 154 us
  local copies, waits for them, and re-layouts: 85.4 us -> 0 us
  blocking collectives: 78 us -> 0 us
  other arithmetic: 63.3 us -> 0 us
  between operations: 15.8 us -> 0.84 us
    dot_general x47 -> x0, matrix products: 228 us -> none  [the longest x4 56.7 us: one_sequence(): jnp.einsum('hqk,qhe->khe', grad_scores, q_block, preferred_element_type=j...]
    pallas_call x0 -> x2, Pallas kernels: none -> 154 us  [the longest x1 145 us: fused_block(): pl.pallas_call(functools.partial(block_kernel, n_bits), out_shape=(jax.Sh...]
    reduce_scatter x4 -> x0, waiting for transfers between devices: 134 us -> none  [the longest x1 38.1 us: body(): lax.psum_scatter(jnp.einsum('tf,df->td', lax.slice_in_dim(grad_pre_low, 0...]
    psum x1 -> x0, waiting for transfers between devices: 119 us -> none  [reduce_low(): return lax.psum(values.astype(jnp.bfloat16), 'wide').astype(jnp.float32)]
    all_gather x4 -> x0, waiting for transfers between devices: 98.3 us -> none  [the longest x1 28.6 us: body(): lax.all_gather(grad_branch.astype(jnp.bfloat16), 'narrow', axis=0, tiled=...]
    psum x2 -> x0, blocking collectives: 34 us -> none  [the longest x1 22.5 us: reduce_low(): return lax.psum(values.astype(jnp.bfloat16), 'wide').astype(jnp.float32)]
    unnamed x183 -> x0, local copies, waits for them, and re-layouts: 33.3 us -> none
    all_gather x1 -> x0, blocking collectives: 30.9 us -> none  [body(): all_modulation = lax.all_gather(grad_modulation, 'wide', axis=0, tiled=True)]
  transfers between devices with their start and end apart: 9 -> 0, of which waited for: 9 -> 0; matrix products, arithmetic and copies ran while one was open for 5% -> 0% of each run, Pallas kernels for 0% -> 0%
where the time goes in v2:
time: 155 us
  Pallas kernels  154 us (99%)
    pallas_call x1, Pallas kernels, fused_block(): pl.pallas_call(functools.partial(block_kernel, n_bits), out_shape=(jax.Sh...  145 us
    pallas_call x1, Pallas kernels, finish(): pl.pallas_call(finish_kernel, out_shape=tuple((jax.ShapeDtypeStruct(shape...  9.17 us

profile of v2, /device:TPU:0, one launch (start us, length us, event | category | flops | bytes accessed | tf_op | source)
XLA Modules:
  0.0 155.2 jit_solution(1404083828283667127)
XLA Ops:
  0.6 145.2 %shard_map.264 = (bf16[512,768]{1,0:T(8,128)(2,1)}, f32[512,768]{1,0:T(8,128)}, bf16[2,2,16,8,384]{4,3,2,1,0:T(8,128)(2,1)}, bf16[2304,768]{1,0:T(8,128)(2,1)}) custom-call(bf16[512,768]{1,0:T(8,128)(2,1)} %tok_in.1, bf16[512,768]{1,0:T(8,128)(2,1)} %cot_in.1, s32[512]{0:T(512)} %mask_in.1, s32[2]{0:T(128)} %step_in.1, f32[1000,128]{1,0:T(8,128)} %table_in.3, ...), custom_call_target="tpu_custom_call" | custom-call | tf_op jit(solution)/shard_map/pallas_call | solution.py:964
  145.8 9.2 %shard_map.265 = (bf16[512,768]{1,0:T(8,128)(2,1)}, f32[512,768]{1,0:T(8,128)}, f32[1000,128]{1,0:T(8,128)}, f32[128,4608]{1,0:T(8,128)}, f32[4608]{0:T(1024)}, ...) custom-call(bf16[2,2,16,8,384]{4,3,2,1,0:T(8,128)(2,1)} %get-tuple-e, ...), custom_call_target="tpu_custom_call" | custom-call | tf_op jit(solution)/shard_map/pallas_call | solution.py:1070

commit v3 on v2

--- a/solution.py
+++ b/solution.py
@@ -35,35 +35,39 @@
     "u1": (960, 192),
     "u2": (1152, 192),
     "u3": (1344, 192),
-    "o": (1536, 192),
-    "q": (1728, 192),
-    "k": (1920, 192),
-    "v": (2112, 192),
+    "o0": (1536, 192),
+    "q0": (1728, 192),
+    "q1": (1920, 192),
+    "q2": (2112, 96),
+    "q3": (2208, 96),
 }
 ORDERS = {
-    "d0": (1, 0, "y", 2),
-    "d1": (1, 0, "y", 2),
-    "d2": (0, 1, "y", 2),
-    "d3": ("y", 0, 1, 2),
-    "u0": ("y", 0, 1, 2),
-    "u1": (0, 1, "y", 2),
-    "u2": (0, 1, "y", 2),
-    "u3": ("y", 0, 1, 2),
-    "o": (0, 1, "y", 2),
-    "q": (0, "y", 1, 2),
-    "k": ("y", 0, 1, 2),
-    "v": ("y", 1, 0, 2),
+    "d0": (0, "y", "Z"),
+    "d1": (0, "y", "Z"),
+    "d2": ("y", 0, "Z"),
+    "d3": ("y", 0, "Z"),
+    "u0": (1, 0, "y", 2),
+    "u1": ("y", 0, "Z"),
+    "u2": (1, "y", 0, 2),
+    "u3": (0, "y", 1, 2),
+    "o0": ("y", 0, "Z"),
+    "q0": ("y", 0, "Z"),
+    "q1": ("y", 0, 1, 2),
+    "q2": ("y", 0, "Z"),
+    "q3": ("y", 0, "Z"),
 }
 PIECES = {
-    "q": (0, 1, 0, 1, 0, 1,),
-    "o": (0,),
-    "u": (1, 0, 1, 0,),
-    "d": (1, 0, 1, 0,),
+    "q": (3, 2, 1,),
+    "o": (2,),
+    "u": (0, 3, 3, 2,),
+    "d": (0, 1,),
 }
+LATE_OUT = False
 PLACES = (
     "n0", "n1", "p0", "p1", "a0", "a1", "a2", "wq", "p2", "p3", "a3", "a4", "a5", "wo", "o0", "o1", "u3",
-    "wu", "u4", "u5", "u6", "u7", "f0", "f1", "f2", "wd", "f3", "f4", "f5", "f6", "f7", "f8", "h0", "h1",
-    "h2", "b0", "b1", "b2", "bx", "b3", "b4", "b5", "by", "g0", "g1", "g2", "g3",
+    "v0", "v1", "wu", "u4", "u5", "u6", "u7", "f0", "f1", "wd", "f3", "f4", "f5", "f6", "h0", "h1", "i0",
+    "b0", "i1", "b1", "i2", "b2", "bx", "i3", "b3", "i4", "b4", "i5", "b5", "by", "c0", "g0", "c1", "g1",
+    "g2", "g3",
 )
 SCHEDULE = {
     "n1": (
@@ -76,95 +80,96 @@
         "Wq2",
     ),
     "a1": (
-        "Wq3",
-    ),
-    "a2": (
-        "Wq4", "Wq5",
+        "Wq0", "Wq1", "Wo0",
     ),
     "p2": (
-        "Wo0",
+        "Wu0", "Wo0", "Wu1",
+    ),
+    "p3": (
+        "Wu2",
     ),
     "a3": (
-        "Wu0",
+        "Wu3",
     ),
     "a5": (
         "Wu1",
     ),
+    "o0": (
+        "Wu2",
+    ),
     "o1": (
-        "Wu2",
+        "Wd0",
     ),
     "u3": (
-        "Wu3", "Wd0",
-    ),
-    "u4": (
+        "Wu3",
+    ),
+    "v1": (
         "Wd1",
     ),
-    "u5": (
-        "Wd2",
-    ),
     "f0": (
-        "Wd3", "d3",
-    ),
-    "f1": (
-        "d2", "d1", "d0",
-    ),
-    "f4": (
-        "u0", "u3", "d3",
+        "d1", "d2", "d3", "d0",
     ),
     "f5": (
-        "u2", "u1", "d1",
-    ),
-    "f6": (
-        "d2",
-    ),
-    "f7": (
-        "u0", "d3", "d0",
-    ),
-    "f8": (
-        "d2",
+        "u0", "d1", "d2", "u3", "u2", "u1",
     ),
     "h0": (
-        "u2", "d3",
+        "d3", "d0",
     ),
     "h1": (
-        "u3", "o",
-    ),
-    "b0": (
-        "d2", "u2", "re", "u1",
+        "o0",
+    ),
+    "i0": (
+        "u0", "d1", "d2",
     ),
     "b1": (
-        "u2", "re", "d3", "d1",
+        "u3", "u1",
+    ),
+    "i2": (
+        "u2",
     ),
     "b2": (
-        "d2", "u0", "u1", "d1",
+        "d1", "d3", "d0",
     ),
     "bx": (
-        "k", "v", "d0", "u2", "d3",
+        "q2", "q3", "q0", "q1",
+    ),
+    "i3": (
+        "u0", "d2",
     ),
     "b3": (
-        "d2", "u0", "u3", "u1",
+        "d1", "o0", "u1",
+    ),
+    "i4": (
+        "d3",
     ),
     "b4": (
-        "u2", "d1", "o", "re",
+        "d2", "u3", "d0",
+    ),
+    "i5": (
+        "d1", "o0",
     ),
     "b5": (
-        "u0", "u3", "d3",
+        "d3", "u2", "u1",
     ),
     "by": (
-        "k", "u1", "q", "o",
+        "q2", "d2",
+    ),
+    "c0": (
+        "d1", "u3", "d0",
     ),
     "g0": (
-        "d2", "re", "u0", "v", "d0",
+        "q2", "q3", "o0", "d3", "u2", "u1",
     ),
     "g1": (
-        "u2", "u3", "u1", "o", "d1",
+        "d2", "u3",
     ),
     "g2": (
-        "re", "rl",
+        "re", "q0", "rl", "q2", "d0", "q3",
     ),
     "g3": (
-        "k", "v", "re", "rl", "d0", "u3", "q", "o", "d1", "u0", "k", "q", "o", "u1", "v", "rl", "k", "q", "d0",
-        "rl", "v", "u3", "k", "o", "q", "v", "d0", "rl", "q", "k", "rl", "v", "q",
+        "o0", "d3", "u2", "q1", "q0", "q2", "u1", "u0", "re", "u3", "rl", "d0", "q3", "u2", "o0", "q2", "q0",
+        "q1", "u0", "u1", "q3", "u2", "re", "q1", "q0", "u3", "rl", "re", "q3", "o0", "q1", "q2", "q0", "rl",
+        "u0", "re", "q3", "q1", "re", "rl", "q0", "rl", "u0", "q1",
     ),
 }
 
@@ -173,11 +178,15 @@
     rows = CHUNKS[name][1]
     out = []
     before_y = True
-    order = [dim for dim in ORDERS[name] if dim == "y" or dim < n_bits]
-    for dim in order + list(range(3, n_bits)):
+    order = [dim for dim in ORDERS[name] if dim != "Z"] + list(range(3, n_bits))
+    if "Z" in ORDERS[name]:
+        order.append("Z")
+    for dim in order:
         if dim == "y":
             out.append((dim, False, rows, False))
             before_y = False
+        elif dim == "Z":
+            out += [("Z1", False, rows, False), ("Z2", False, rows, False), ("Z3", False, rows, False)]
         else:
             halved = rows % 32 == 0
             rows = rows // 2 if halved else rows
@@ -185,16 +194,24 @@
     return out
 
 
-def stage_rows(index, n_bits):
-    total = 0
-    for name in CHUNKS:
-        _, _, rows, both = chunk_stages(name, n_bits)[index]
-        total += 2 * rows if both else rows
-    return total
+def recv_rows(n_bits):
+    return sum(
+        2 * rows if both else rows for name in CHUNKS for _, _, rows, both in chunk_stages(name, n_bits)
+    )
 
 
 def outbox_rows(n_bits):
     return sum(rows for name in CHUNKS for _, halved, rows, both in chunk_stages(name, n_bits) if halved and both)
+
+
+def remote_count(n_bits):
+    count = 15 + 2 * (n_bits + 3)
+    for matrix in PIECES:
+        count += sum(2 if kind < 2 else 4 for kind in PIECES[matrix])
+    for name in CHUNKS:
+        for _, halved, _, both in chunk_stages(name, n_bits):
+            count += (2 if both else 1) + (1 if halved else 0)
+    return count
 
 
 def dot(left, right, dims):
@@ -236,7 +253,7 @@
     tok, cot, gb, n2, normed, wqkv, wout, wup, wdown, proj, ho, do, lse, attn, mid, part, hidden, gel,
     grad_mid, send_a, recv_a, recv_b, recv_c, acc, oth, stage,
     mod, vec, bup, ada_line, lines, mask_line, cos_t, sin_t, sums, sums_recv, sums_low,
-    ssem, rsem, lsem, *stage_recv,
+    ssem, rsem, lsem, stage_recv, table, w_ada,
 ):
     wide = lax.axis_index("wide")
     narrow = lax.axis_index("narrow")
@@ -251,7 +268,10 @@
     def wide_peer(level):
         return (wide + (1 << level) * (1 - 2 * wide_bit(level)), narrow)
 
-    peers = [sib, across] + [wide_peer(level) for level in range(n_bits)]
+    bit_lo, bit_hi = wide_bit(1), wide_bit(2)
+    at_end = bit_lo == bit_hi
+    inner_peer = (wide + 2 * (1 - 2 * bit_lo) + 4 * (1 - 2 * bit_hi), narrow)
+    peers = [sib, across, inner_peer] + [wide_peer(level) for level in range(n_bits)]
     own0 = core * ROWS_LOCAL
     sib0 = (1 - core) * ROWS_LOCAL
 
@@ -282,12 +302,13 @@
         local(cos_in, cos_t),
         local(sin_in, sin_t),
     ]
+    c_ada = [local(table_in, table), local(w_ada_in, w_ada)]
     c_wqkv = local(wqkv_in, wqkv.at[0])
     c_wout = local(wout_in, wout.at[pl.ds(0, 192)])
     c_wup = local(wup_in, wup.at[:, pl.ds(0, D)])
     c_wdown = local(wdown_in, wdown.at[pl.ds(0, D)])
     c_tok.start()
-    for copy in c_small:
+    for copy in c_small + c_ada:
         copy.start()
     c_wqkv.start()
     c_cot.start()
@@ -310,30 +331,50 @@
         "u": (wup_in, lambda rows: wup.at[rows, pl.ds(D, D)], D, 0),
         "d": (wdown_in, lambda rows: wdown.at[rows], D, D),
     }
-    w_across, w_along, plans = {}, {}, {}
+    w_across, w_sent, w_last, plans = {}, {}, {}, {}
     piece_keys = []
+    ahead = 6
+
+    def pass_on(at, arrived, copies):
+        arrived.wait_recv()
+        for copy in copies:
+            copy.start()
+        if at is not None and at + ahead < len(piece_keys):
+            w_across[piece_keys[at + ahead]].start()
+
     for matrix in PIECES:
         source, target, total_rows, shift = places[matrix]
         count = len(PIECES[matrix])
-        size = total_rows // (2 * count)
         for piece in range(count):
-            level = PIECES[matrix][piece]
-            row = 2 * size * piece + wide_bit(level) * size
-            here = target(rows_at(shift + row, size, 16))
+            kind = PIECES[matrix][piece]
+            at = len(piece_keys)
             key = "W" + matrix + str(piece)
             piece_keys.append(key)
+            first = piece * (total_rows // count)
+            if kind < 2:
+                size = total_rows // (2 * count)
+                row = first + wide_bit(kind) * size
+                here = target(rows_at(shift + row, size, 16))
+                along = remote(here, here, wide_peer(kind))
+                w_sent[key], w_last[key] = [along], [along]
+                steps = [(at, [along])]
+            else:
+                size = total_rows // (4 * count)
+                bits = (wide_bit(0), wide_bit(1))
+
+                def quarter(bit_0, bit_1):
+                    return target(rows_at(shift + first + (2 * bit_0 + bit_1) * size, size, 16))
+
+                row = first + (2 * bits[0] + bits[1]) * size
+                here = quarter(*bits)
+                along = [remote(here, here, wide_peer(level)) for level in (0, 1)]
+                theirs = quarter(1 - bits[0], bits[1]) if kind == 2 else quarter(bits[0], 1 - bits[1])
+                last = remote(theirs, theirs, wide_peer(3 - kind))
+                w_sent[key], w_last[key] = along + [last], [along[3 - kind], last]
+                steps = [(at, along), (along[kind - 2], [last])]
             w_across[key] = remote(source.at[rows_at(row, size, 16)], here, across)
-            w_along[key] = remote(here, here, wide_peer(level))
-    ahead = 6
-
-    def forward_piece(at):
-        w_across[piece_keys[at]].wait_recv()
-        w_along[piece_keys[at]].start()
-        if at + ahead < len(piece_keys):
-            w_across[piece_keys[at + ahead]].start()
-
-    for at, key in enumerate(piece_keys):
-        plans[key] = [functools.partial(forward_piece, at)]
+            plans[key] = [functools.partial(pass_on, at, w_across[key], steps[0][1])]
+            plans[key] += [functools.partial(pass_on, None, arrived, copies) for arrived, copies in steps[1:]]
     r_bup = remote(bup_in, bup[1], across)
     for key in piece_keys[:ahead]:
         w_across[key].start()
@@ -349,22 +390,22 @@
 
     stage_copies, back_copies, stage_base, returns, final_copies, outbox = {}, {}, {}, {}, {}, {}
     stage_rows_used = 0
-    n_stages = n_bits + 1
-    for index in range(n_stages):
-        base = 0
-        for name in CHUNKS:
-            dim, halved, count, both = chunk_stages(name, n_bits)[index]
+    base = 0
+    for name in CHUNKS:
+        for index, (dim, halved, count, both) in enumerate(chunk_stages(name, n_bits)):
             offset, _ = segment(name, index)
             stage_base[name, index] = base
             if dim == "y":
                 sent, peer = [oth], across
+            elif dim in ("Z1", "Z2", "Z3"):
+                sent, peer = [acc], inner_peer if dim == "Z2" else wide_peer(1)
             else:
                 sent, peer = [acc, oth] if both else [acc], wide_peer(dim)
                 if halved:
                     offset = offset + (1 - wide_bit(dim)) * count
             copies = []
             for array in sent:
-                landing = stage_recv[index].at[pl.ds(base, count)]
+                landing = stage_recv.at[pl.ds(base, count)]
                 source = array.at[rows_at(offset, count, 16)]
                 if halved and array is acc:
                     if both:
@@ -382,7 +423,7 @@
                 rows = acc.at[rows_at(offset, count, 16)]
                 back_copies[name, index] = remote(rows, rows, peer)
     for name in CHUNKS:
-        returns[name] = [at for at in range(n_stages) if (name, at) in back_copies]
+        returns[name] = [at for at in range(len(chunk_stages(name, n_bits))) if (name, at) in back_copies]
         first, count = CHUNKS[name]
         final_copies[name] = local(acc.at[pl.ds(first, count)], grads_out.at[pl.ds(first, count)])
 
@@ -396,14 +437,14 @@
             copy.start()
 
     def merge_step(name, index):
-        for copy in stage_copies[name, index - 1]:
-            copy.wait()
+        stages = chunk_stages(name, n_bits)
+        before = stages[index - 1][0]
+        copies = stage_copies[name, index - 1]
         offset, rows = segment(name, index)
-        both_before = len(stage_copies[name, index - 1]) == 2
+        both_before = len(copies) == 2
         base = stage_base[name, index - 1]
-        brought = stage_recv[index - 1]
-
-        def merge(array, row0, count, box=None):
+
+        def merge(array, row0, count, box=None, replace=False):
             start = base + rows if array is oth else base
             step = 48 if count % 48 == 0 else 16
             target, target0 = box or (array, row0)
@@ -411,22 +452,74 @@
             def one(at):
                 row = row0 + step * at
                 here = rows_at(row, step, 16)
-                value = array[here, :].astype(f32) + brought[rows_at(start + row - offset, step, 16), :].astype(f32)
-                target[rows_at(target0 + step * at, step, 16), :] = value.astype(bf16)
+                value = stage_recv[rows_at(start + row - offset, step, 16), :]
+                if not replace:
+                    value = (array[here, :].astype(f32) + value.astype(f32)).astype(bf16)
+                target[rows_at(target0 + step * at, step, 16), :] = value
 
             loop(count // step, one)
 
+        def go_on():
+            if index == len(stages):
+                back_copies[name, returns[name][-1]].start()
+            else:
+                start_stage(name, index)
+
+        if before == "Z1":
+
+            @pl.when(at_end)
+            def _():
+                copies[0].wait_send()
+
+            @pl.when(jnp.logical_not(at_end))
+            def _():
+                copies[0].wait_recv()
+                merge(acc, offset, rows)
+                go_on()
+
+            return
+        if before == "Z2":
+
+            @pl.when(jnp.logical_not(at_end))
+            def _():
+                copies[0].wait()
+                merge(acc, offset, rows)
+                go_on()
+
+            return
+        if before == "Z3":
+
+            @pl.when(at_end)
+            def _():
+                copies[0].wait_recv()
+                merge(acc, offset, rows, replace=True)
+
+            @pl.when(jnp.logical_not(at_end))
+            def _():
+                copies[0].wait_send()
+
+            go_on()
+            return
+        for copy in copies:
+            copy.wait()
         arrays = [acc, oth] if both_before else [acc]
-        if index == n_stages:
+        if index == len(stages):
             merge(acc, offset, rows)
-            back_copies[name, returns[name][-1]].start()
+            go_on()
             return
-        dim, halved, count, _ = chunk_stages(name, n_bits)[index]
+        dim, halved, count, _ = stages[index]
         if dim == "y":
             for array in reversed(arrays):
                 merge(array, offset, rows)
                 if array is oth or not both_before:
                     start_stage(name, index)
+        elif dim == "Z1":
+            merge(acc, offset, rows)
+
+            @pl.when(at_end)
+            def _():
+                start_stage(name, index)
+
         elif halved:
             for array in arrays:
                 box = outbox[name, index] if array is acc else None
@@ -447,7 +540,7 @@
 
     for name in CHUNKS:
         plan = [functools.partial(start_stage, name, 0)]
-        plan += [functools.partial(merge_step, name, index + 1) for index in range(n_stages)]
+        plan += [functools.partial(merge_step, name, index + 1) for index in range(len(chunk_stages(name, n_bits)))]
         plan += [functools.partial(back_step, name, at) for at in reversed(range(len(returns[name])))]
         plans[name] = plan
 
@@ -502,7 +595,8 @@
         point("w" + matrix)
         for key in piece_keys:
             if key[1] == matrix:
-                w_along[key].wait_recv()
+                for copy in w_last[key]:
+                    copy.wait_recv()
 
     for copy in c_small:
         copy.wait()
@@ -510,20 +604,14 @@
     for row in range(3):
         vec[row : row + 1, :] = lines[row][...].reshape(1, D)
 
-    def modulation(table, w_ada):
-        copies = [local(table_in, table), local(w_ada_in, w_ada)]
-        for copy in copies:
-            copy.start()
-        for copy in copies:
-            copy.wait()
-        picked = table[pl.ds(time_step, 1), :]
-        cond = picked / (1.0 + jnp.exp(-picked))
-        cond = jnp.broadcast_to(cond, (16, 128)).astype(bf16)
-        for index in range(6):
-            flat = dot(cond, w_ada[:, index * D : (index + 1) * D], NN)
-            mod[index : index + 1, :] = ada_line[pl.ds(index * D, D)].reshape(1, D) + flat[0:1, :]
-
-    pl.run_scoped(modulation, pltpu.VMEM((1000, 128), f32), pltpu.VMEM((128, 6 * D), bf16))
+    for copy in c_ada:
+        copy.wait()
+    picked = table[pl.ds(time_step, 1), :]
+    cond = picked / (1.0 + jnp.exp(-picked))
+    cond = jnp.broadcast_to(cond, (16, 128)).astype(bf16)
+    for index in range(6):
+        flat = dot(cond, w_ada[:, index * D : (index + 1) * D], NN)
+        mod[index : index + 1, :] = ada_line[pl.ds(index * D, D)].reshape(1, D) + flat[0:1, :]
 
     def first_norm(source, src0, dst0):
         def one(index):
@@ -661,19 +749,11 @@
         vec[4 + row : 5 + row, :] = bup[row][...].reshape(1, D)
     gelu_c = math.sqrt(2.0 / math.pi)
 
-    def up(index):
-        shard = lax.div(index, 4)
-        block = lax.rem(index, 4)
-
-        @pl.when(index == 2)
+    def up(shard, block):
+        @pl.when((shard == 0) & (block == 2))
         def _():
             r_n2[0].wait_recv()
             r_n2[1].wait_recv()
-
-        @pl.when(index == 4)
-        def _():
-            point("u3")
-            need("u")
 
         rows = rows_at(lax.rem(own0 + 256 * block, LEN), 256, 256)
         cols = rows_at(shard * D, D, D)
@@ -685,9 +765,8 @@
         slope = gate + 0.5 * pre * (1.0 - squash * squash) * (gelu_c * (1.0 + 3.0 * 0.044715 * square))
         gel[rows, cols] = slope.astype(bf16)
 
-        point_in("u", index, True, 8)
-
-    loop(8, up)
+    loop(4, functools.partial(up, 0))
+    point("u3")
 
     def w_down_grad(shard, target, base):
         def one(index):
@@ -697,11 +776,8 @@
 
         loop(3, one)
 
-    w_down_grad(1, oth, 0)
-    point("f0")
     w_down_grad(0, acc, 0)
-    point("f1")
-
+    point("v0")
     sums[...] = jnp.zeros_like(sums)
     c_wdown.wait()
 
@@ -726,14 +802,21 @@
         loop(3, one)
 
     hidden_grad(0, 3 + narrow)
-    point("f2")
+    point("v1")
+    need("u")
+
+    def up_other(block):
+        up(1, block)
+        point_in("u", block + 4, True, 8)
+
+    loop(4, up_other)
+    w_down_grad(1, oth, 0)
+    point("f0")
+    w_up_grad(0, acc)
+    point("f1")
     need("d")
     hidden_grad(1, 3 + lax.rem(narrow + 2, 4))
     point("f3")
-    w_up_grad(1, oth)
-    point("f4")
-    w_up_grad(0, acc)
-    point("f5")
 
     r_gn2 = []
     for index in range(2):
@@ -743,7 +826,9 @@
     for index in range(2):
         out = dot(gel[rows_at(own0 + half * index, half, half), :], wup[...], NT)
         part[half * index : half * (index + 1), :] = out
-    point("f6")
+    point("f4")
+    w_up_grad(1, oth)
+    point("f5")
 
     r_ga = []
     for index in range(2):
@@ -772,7 +857,76 @@
         rows = rows_at(own0 + half * index, half, half)
         r_ga.append(remote(gb.at[rows], gb.at[rows], sib))
         r_ga[index].start()
-    point("f7")
+    point("f6")
+
+    r_ga[0].wait_recv()
+    r_ga[1].wait_recv()
+
+    def head_grad(index):
+        cols = rows_at(256 * index, 256, 256)
+        do[:, cols] = dot(wout[...], gb[cols, :], NT).astype(bf16)
+
+    loop(4, head_grad)
+    point("h0")
+
+    def w_out_grad():
+        oth[1536:1728, :] = dot(ho[192:384, :], gb[...], NN).astype(bf16)
+        acc[1536:1728, :] = dot(ho[0:192, :], gb[...], NN).astype(bf16)
+        point("h1")
+
+    if not LATE_OUT:
+        w_out_grad()
+
+    def attend_back(shard, head, between):
+        q_t = proj[shard, head_rows(0, head), :]
+        k_t = proj[shard, head_rows(1, head), :]
+        v_t = proj[shard, head_rows(2, head), :]
+        index = shard * SHARD_HEADS + head
+        d_t = do[rows_at(index * HD, HD, HD), :]
+        probs = jnp.exp(dot(k_t, q_t, TN) - lse[index, 0:1, :])
+        grad_probs = dot(v_t, d_t, TN)
+        inner = jnp.sum(probs * grad_probs, axis=0, keepdims=True)
+        grad_scores = (probs * (grad_probs - inner)).astype(bf16)
+        between()
+        dq_t = dot(k_t, grad_scores, NN) * 0.125
+        dk_t = dot(grad_scores, q_t, NT).T
+        dv_t = dot(probs.astype(bf16), d_t, NT).T
+        for kind, grad in ((0, dq_t), (1, dk_t)):
+            low, high = grad[:32], grad[32:]
+            turned = jnp.concatenate(
+                [low * cos_t[...] + high * sin_t[...], high * cos_t[...] - low * sin_t[...]], axis=0
+            )
+            proj[shard, head_rows(kind, head), :] = turned.astype(bf16)
+        proj[shard, head_rows(2, head), :] = dv_t.astype(bf16)
+
+    for key in piece_keys:
+        for copy in w_sent[key] + [w_across[key]]:
+            copy.wait_send()
+
+    def w_qkv_grad(shard, target):
+        def one(index):
+            rows = rows_at(192 * index, 192, 64)
+            out = dot(proj[shard, rows, :], normed[...], NN)
+            target[rows_at(1728 + 192 * index, 192, 64), :] = out.astype(bf16)
+
+        loop(3, one)
+
+    def back_heads(index):
+        shard = 1 - lax.div(index, SHARD_HEADS)
+        head = lax.rem(index, SHARD_HEADS)
+        attend_back(shard, head, lambda: point_in("i", index, True, 6))
+        point_in("b", index, True, 6)
+
+        @pl.when(index == 2)
+        def _():
+            w_qkv_grad(1, oth)
+            point("bx")
+
+    loop(6, back_heads)
+    w_qkv_grad(0, acc)
+    point("by")
+    if LATE_OUT:
+        w_out_grad()
 
     r_branch = []
     for index in range(2):
@@ -782,20 +936,22 @@
     for index in range(2):
         out = dot(hidden[rows_at(own0 + half * index, half, half), :], wdown[...], NN)
         part[half * index : half * (index + 1), :] = out
-    point("f8")
-
-    r_ga[0].wait_recv()
-    r_ga[1].wait_recv()
-
-    def head_grad(index):
-        cols = rows_at(256 * index, 256, 256)
-        do[:, cols] = dot(wout[...], gb[cols, :], NT).astype(bf16)
-
-    loop(4, head_grad)
-    point("h0")
-    oth[1536:1728, :] = dot(ho[192:384, :], gb[...], NN).astype(bf16)
-    acc[1536:1728, :] = dot(ho[0:192, :], gb[...], NN).astype(bf16)
-    point("h1")
+    point("c0")
+
+
+    def normed_grad(offset):
+        first = dot(proj[0, :, offset], wqkv[0], TN)
+        return first + dot(proj[1, :, offset], wqkv[1], TN)
+
+    r_gn = []
+    for index in range(2):
+        rows = pl.ds(half * index, half)
+        recv_b[rows, :] = normed_grad(rows_at(sib0 + half * index, half, half)).astype(bf16)
+        r_gn.append(remote(recv_b.at[rows], recv_a.at[rows], sib))
+        r_gn[index].start()
+    for index in range(2):
+        attn[half * index : half * (index + 1), :] = normed_grad(rows_at(own0 + half * index, half, half))
+    point("g0")
 
     def finish_branch(index):
         rows = rows_at(128 * index, 128, 128)
@@ -813,100 +969,35 @@
     sums[0, 6:7, :] = jnp.full((1, D), high.astype(f32) * on_first)
     sums[0, 7:8, :] = jnp.full((1, D), (time_step - 32 * high).astype(f32) * on_first)
     r_sib[0].start()
-    point("h2")
-
-    def attend_back(shard, head):
-        q_t = proj[shard, head_rows(0, head), :]
-        k_t = proj[shard, head_rows(1, head), :]
-        v_t = proj[shard, head_rows(2, head), :]
-        index = shard * SHARD_HEADS + head
-        d_t = do[rows_at(index * HD, HD, HD), :]
-        probs = jnp.exp(dot(k_t, q_t, TN) - lse[index, 0:1, :])
-        grad_probs = dot(v_t, d_t, TN)
-        inner = jnp.sum(probs * grad_probs, axis=0, keepdims=True)
-        grad_scores = (probs * (grad_probs - inner)).astype(bf16)
-        dq_t = dot(k_t, grad_scores, NN) * 0.125
-        dk_t = dot(grad_scores, q_t, NT).T
-        dv_t = dot(probs.astype(bf16), d_t, NT).T
-        for kind, grad in ((0, dq_t), (1, dk_t)):
-            low, high = grad[:32], grad[32:]
-            turned = jnp.concatenate(
-                [low * cos_t[...] + high * sin_t[...], high * cos_t[...] - low * sin_t[...]], axis=0
-            )
-            proj[shard, head_rows(kind, head), :] = turned.astype(bf16)
-        proj[shard, head_rows(2, head), :] = dv_t.astype(bf16)
-
-    for key in piece_keys:
-        w_along[key].wait_send()
-        w_across[key].wait_send()
-
-    def w_qkv_grad(shard, target):
-        def one(index):
-            rows = rows_at(192 * index, 192, 64)
-            out = dot(proj[shard, rows, :], normed[...], NN)
-            target[rows_at(1728 + 192 * index, 192, 64), :] = out.astype(bf16)
-
-        loop(3, one)
-
-    def back_heads(index):
-        shard = 1 - lax.div(index, SHARD_HEADS)
-        head = lax.rem(index, SHARD_HEADS)
-        attend_back(shard, head)
-
-        @pl.when(index == 0)
-        def _():
-            sums_ready(0)
-
-        point_in("b", index, True, 6)
-
-        @pl.when(index == 2)
-        def _():
-            w_qkv_grad(1, oth)
-            point("bx")
-
-    loop(6, back_heads)
-    w_qkv_grad(0, acc)
-    point("by")
-
-    def normed_grad(offset):
-        first = dot(proj[0, :, offset], wqkv[0], TN)
-        return first + dot(proj[1, :, offset], wqkv[1], TN)
-
-    c_mixed.wait()
-    r_gn = []
-    for index in range(2):
-        send_a[half * index : half * (index + 1), :] = normed_grad(
-            rows_at(sib0 + half * index, half, half)
-        ).astype(bf16)
-        r_gn.append(exchange_start(recv_a, index))
-    for index in range(2):
-        part[half * index : half * (index + 1), :] = normed_grad(rows_at(own0 + half * index, half, half))
-    point("g0")
+    point("c1")
+
     for index in range(2):
         r_gn[index].wait()
 
         def first_back(sub):
             rows = rows_at(half * index + 128 * sub, 128, 128)
-            upstream = part[rows, :] + recv_a[rows, :].astype(f32)
+            upstream = attn[rows, :] + recv_a[rows, :].astype(f32)
             vhat, inverse = normalize(tok[rows, :].astype(f32))
             scaled = upstream * (1.0 + mod[1:2, :])
-            part[rows, :] = grad_mid[rows, :] + norm_grad(vhat, inverse, scaled * vec[0:1, :])
+            attn[rows, :] = grad_mid[rows, :] + norm_grad(vhat, inverse, scaled * vec[0:1, :])
             add_sum(1, 0, upstream)
             add_sum(1, 1, upstream * (vhat * vec[0:1, :]))
             add_sum(1, 2, scaled * vhat)
 
         loop(2, first_back)
-    c_grad_tok = local(part, grad_tok_out)
+    c_grad_tok = local(attn, grad_tok_out)
     c_grad_tok.start()
 
     r_sib[1].start()
     point("g1")
+    sums_ready(0)
     sums_ready(1)
     point("g2")
     point("g3")
     for name in CHUNKS:
         final_copies[name].wait()
     c_grad_tok.wait()
+    c_mixed.wait()
     for copy in [r_tok, r_bup] + r_n2 + r_ga:
         copy.wait_send()
 
@@ -953,12 +1044,13 @@
         pltpu.VMEM((2, 8, D), f32),
         pltpu.VMEM((2, 8, D), f32),
         pltpu.VMEM((2, 8, D // 2), bf16),
-        pltpu.SemaphoreType.DMA((240,)),
-        pltpu.SemaphoreType.DMA((240,)),
-        pltpu.SemaphoreType.DMA((48,)),
+        pltpu.SemaphoreType.DMA((remote_count(n_bits),)),
+        pltpu.SemaphoreType.DMA((remote_count(n_bits),)),
+        pltpu.SemaphoreType.DMA((20 + len(CHUNKS),)),
+        pltpu.VMEM((recv_rows(n_bits), D), bf16),
+        pltpu.VMEM(table.shape, f32),
+        pltpu.VMEM(w_ada.shape, bf16),
     ]
-    for index in range(n_bits + 1):
-        scratch.append(pltpu.VMEM((stage_rows(index, n_bits), D), bf16))
     specs = [any_space] * 17
     specs[3] = pl.BlockSpec(memory_space=pltpu.SMEM)
     return pl.pallas_call(
@@ -1007,8 +1099,17 @@
                 wide_out.at[rows], target.at[pl.ds(192 * piece - first, 192)], sem.at[7 + pieces + piece]
             )
         )
-    for copy in loads + pass_in + grad_in:
+    for copy in grad_in[: pieces // 2] + loads + pass_in + grad_in[pieces // 2 :]:
         copy.start()
+
+    def widen(piece):
+        grad_in[piece].wait()
+        rows = pl.ds(192 * piece, 192)
+        wide_out[rows, :] = grads[rows, :].astype(f32)
+        grad_out[piece].start()
+
+    for piece in range(pieces // 2):
+        widen(piece)
     for copy in loads:
         copy.wait()
 
@@ -1047,14 +1148,11 @@
     table_out[...] = lax.dot_general(pick, grad_cond, TN, precision=highest, preferred_element_type=f32)
     out_table = pltpu.make_async_copy(table_out, g_table, sem.at[7 + 2 * pieces + 6])
     out_table.start()
+    for piece in range(pieces // 2, pieces):
+        widen(piece)
     for at in range(2):
         pass_in[at].wait()
         pass_out[at].start()
-    for piece in range(pieces):
-        grad_in[piece].wait()
-        rows = pl.ds(192 * piece, 192)
-        wide_out[rows, :] = grads[rows, :].astype(f32)
-        grad_out[piece].start()
     for copy in line_out + [out_ada, out_table] + pass_out + grad_out:
         copy.wait()
 

time: 155 us -> 149 us (0.961)
  Pallas kernels: 154 us -> 148 us
    pallas_call x1, Pallas kernels: 145 us -> 139 us  [fused_block(): pl.pallas_call(functools.partial(block_kernel, n_bits), out_shape=(jax.Sh...]
where the time goes in v3:
time: 149 us; the launch traced here: 148 us
  Pallas kernels  148 us (99%)
    pallas_call x1, Pallas kernels, fused_block(): pl.pallas_call(functools.partial(block_kernel, n_bits), out_shape=(jax.Sh...  139 us
    pallas_call x1, Pallas kernels, finish(): pl.pallas_call(finish_kernel, out_shape=tuple((jax.ShapeDtypeStruct(shape...  9.03 us

profile of v3, /device:TPU:0, one launch (start us, length us, event | category | flops | bytes accessed | tf_op | source)
XLA Modules:
  0.0 148.4 jit_solution(16778121725449250118)
XLA Ops:
  0.6 138.5 %shard_map.264 = (bf16[512,768]{1,0:T(8,128)(2,1)}, f32[512,768]{1,0:T(8,128)}, bf16[2,2,16,8,384]{4,3,2,1,0:T(8,128)(2,1)}, bf16[2304,768]{1,0:T(8,128)(2,1)}) custom-call(bf16[512,768]{1,0:T(8,128)(2,1)} %tok_in.1, bf16[512,768]{1,0:T(8,128)(2,1)} %cot_in.1, s32[512]{0:T(512)} %mask_in.1, s32[2]{0:T(128)} %step_in.1, f32[1000,128]{1,0:T(8,128)} %table_in.3, ...), custom_call_target="tpu_custom_call" | custom-call | tf_op jit(solution)/shard_map/pallas_call | solution.py:1056
  139.2 9.0 %shard_map.265 = (bf16[512,768]{1,0:T(8,128)(2,1)}, f32[512,768]{1,0:T(8,128)}, f32[1000,128]{1,0:T(8,128)}, f32[128,4608]{1,0:T(8,128)}, f32[4608]{0:T(1024)}, ...) custom-call(bf16[2,2,16,8,384]{4,3,2,1,0:T(8,128)(2,1)} %get-tuple-e, ...), custom_call_target="tpu_custom_call" | custom-call | tf_op jit(solution)/shard_map/pallas_call | solution.py:1168

commit v4 on v3

--- a/solution.py
+++ b/solution.py
@@ -42,25 +42,25 @@
     "q3": (2208, 96),
 }
 ORDERS = {
-    "d0": (0, "y", "Z"),
+    "d0": (0, "y", 1, 2),
     "d1": (0, "y", "Z"),
     "d2": ("y", 0, "Z"),
     "d3": ("y", 0, "Z"),
-    "u0": (1, 0, "y", 2),
-    "u1": ("y", 0, "Z"),
-    "u2": (1, "y", 0, 2),
-    "u3": (0, "y", 1, 2),
+    "u0": (0, "y", "Z"),
+    "u1": (0, "y", "Z"),
+    "u2": (1, 0, "y", 2),
+    "u3": (1, "y", 0, 2),
     "o0": ("y", 0, "Z"),
     "q0": ("y", 0, "Z"),
-    "q1": ("y", 0, 1, 2),
+    "q1": ("y", 0, "Z"),
     "q2": ("y", 0, "Z"),
     "q3": ("y", 0, "Z"),
 }
 PIECES = {
-    "q": (3, 2, 1,),
-    "o": (2,),
-    "u": (0, 3, 3, 2,),
-    "d": (0, 1,),
+    "q": (3, 2, 0,),
+    "o": (3,),
+    "u": (3, 2, 1, 0,),
+    "d": (2, 2,),
 }
 LATE_OUT = False
 PLACES = (
@@ -80,37 +80,40 @@
         "Wq2",
     ),
     "a1": (
-        "Wq0", "Wq1", "Wo0",
+        "Wq1", "Wq0", "Wo0",
+    ),
+    "a2": (
+        "Wu0",
     ),
     "p2": (
-        "Wu0", "Wo0", "Wu1",
+        "Wu1", "Wo0",
     ),
     "p3": (
         "Wu2",
     ),
     "a3": (
-        "Wu3",
-    ),
-    "a5": (
-        "Wu1",
+        "Wu0",
+    ),
+    "a4": (
+        "Wu3", "Wu1",
     ),
     "o0": (
-        "Wu2",
-    ),
-    "o1": (
         "Wd0",
     ),
     "u3": (
-        "Wu3",
-    ),
-    "v1": (
         "Wd1",
     ),
+    "v0": (
+        "Wd0",
+    ),
+    "u6": (
+        "Wd1",
+    ),
     "f0": (
-        "d1", "d2", "d3", "d0",
+        "d2", "d3", "d1", "d0",
     ),
     "f5": (
-        "u0", "d1", "d2", "u3", "u2", "u1",
+        "u2", "u1", "d2", "d1", "u3", "u0",
     ),
     "h0": (
         "d3", "d0",
@@ -119,57 +122,57 @@
         "o0",
     ),
     "i0": (
-        "u0", "d1", "d2",
-    ),
-    "b1": (
-        "u3", "u1",
+        "u2", "d1",
+    ),
+    "i1": (
+        "u1", "d0",
     ),
     "i2": (
-        "u2",
+        "d2", "u3",
     ),
     "b2": (
-        "d1", "d3", "d0",
+        "d1",
     ),
     "bx": (
-        "q2", "q3", "q0", "q1",
+        "q1", "q3", "o0", "q0", "d0", "q2",
     ),
     "i3": (
-        "u0", "d2",
+        "u1", "u0",
     ),
     "b3": (
-        "d1", "o0", "u1",
+        "d2", "d1",
     ),
     "i4": (
-        "d3",
+        "d3", "u3",
     ),
     "b4": (
-        "d2", "u3", "d0",
+        "d0",
     ),
     "i5": (
-        "d1", "o0",
+        "u2", "u1", "d2", "d1",
     ),
     "b5": (
-        "d3", "u2", "u1",
+        "d3", "o0",
     ),
     "by": (
-        "q2", "d2",
+        "q1", "u3", "d0",
     ),
     "c0": (
-        "d1", "u3", "d0",
+        "u1", "q3", "d2", "d1",
     ),
     "g0": (
-        "q2", "q3", "o0", "d3", "u2", "u1",
+        "q1", "d3", "o0",
     ),
     "g1": (
-        "d2", "u3",
+        "q0", "u3", "d0",
     ),
     "g2": (
-        "re", "q0", "rl", "q2", "d0", "q3",
+        "u1", "re", "rl",
     ),
     "g3": (
-        "o0", "d3", "u2", "q1", "q0", "q2", "u1", "u0", "re", "u3", "rl", "d0", "q3", "u2", "o0", "q2", "q0",
-        "q1", "u0", "u1", "q3", "u2", "re", "q1", "q0", "u3", "rl", "re", "q3", "o0", "q1", "q2", "q0", "rl",
-        "u0", "re", "q3", "q1", "re", "rl", "q0", "rl", "u0", "q1",
+        "q2", "q3", "q1", "o0", "d3", "u0", "d2", "q3", "u2", "re", "rl", "q1", "o0", "q0", "u0", "u3", "q3",
+        "u2", "u1", "q1", "q0", "q2", "u0", "u3", "d3", "re", "rl", "q3", "q2", "q0", "o0", "u0", "re", "q2",
+        "u2", "rl", "q1", "q0", "q3", "re", "q2", "re", "u0", "u2", "q0", "rl", "rl", "q2",
     ),
 }
 
@@ -307,6 +310,9 @@
     c_wout = local(wout_in, wout.at[pl.ds(0, 192)])
     c_wup = local(wup_in, wup.at[:, pl.ds(0, D)])
     c_wdown = local(wdown_in, wdown.at[pl.ds(0, D)])
+    barrier = pltpu.get_barrier_semaphore()
+    for peer in peers:
+        pl.semaphore_signal(barrier, inc=1, device_id=peer, device_id_type=MESH)
     c_tok.start()
     for copy in c_small + c_ada:
         copy.start()
@@ -316,9 +322,6 @@
     c_wup.start()
     c_wdown.start()
 
-    barrier = pltpu.get_barrier_semaphore()
-    for peer in peers:
-        pl.semaphore_signal(barrier, inc=1, device_id=peer, device_id_type=MESH)
     pl.semaphore_wait(barrier, len(peers))
 
     r_tok = remote(tok_in, n2.at[rows_at(own0, ROWS_LOCAL, 512)], sib)
@@ -607,6 +610,7 @@
     for copy in c_ada:
         copy.wait()
     picked = table[pl.ds(time_step, 1), :]
+    vec[3:4, 0:128] = picked
     cond = picked / (1.0 + jnp.exp(-picked))
     cond = jnp.broadcast_to(cond, (16, 128)).astype(bf16)
     for index in range(6):
@@ -966,8 +970,19 @@
     c_mixed.start()
     on_first = (1 - core).astype(f32)
     high = lax.div(time_step, 32)
-    sums[0, 6:7, :] = jnp.full((1, D), high.astype(f32) * on_first)
-    sums[0, 7:8, :] = jnp.full((1, D), (time_step - 32 * high).astype(f32) * on_first)
+    picked = vec[3:4, 0:128]
+    sigma = 1.0 / (1.0 + jnp.exp(-picked))
+    slope = sigma * (1.0 + picked * (1.0 - sigma))
+    slope_high = slope.astype(bf16).astype(f32)
+    entries = [
+        jnp.full((1, 128), high.astype(f32)),
+        jnp.full((1, 128), (time_step - 32 * high).astype(f32)),
+        (picked / (1.0 + jnp.exp(-picked))).astype(bf16).astype(f32),
+        slope_high,
+        slope - slope_high,
+    ]
+    for at, entry in enumerate(entries):
+        sums[0, 6:7, 128 * at : 128 * (at + 1)] = entry * on_first
     r_sib[0].start()
     point("c1")
 
@@ -1065,21 +1080,21 @@
         out_specs=[any_space] * 4,
         scratch_shapes=scratch,
         compiler_params=pltpu.CompilerParams(
-            collective_id=0, has_side_effects=True, vmem_limit_bytes=60 * 1024 * 1024
+            collective_id=0, has_side_effects=True, vmem_limit_bytes=61 * 1024 * 1024
         ),
     )(tokens, cot, mask, timestep, table, w_ada, b_ada, gain_one, w_qkv_t, w_out, gain_two, w_up, b_up, w_down, b_down,
       cos_t, sin_t)
 
 
 def finish_kernel(
-    gathered_in, table_in, w_ada_in, grads_in, mixed_in, grad_tok_in,
+    gathered_in, w_ada_in, grads_in, mixed_in, grad_tok_in,
     mixed_out, grad_tok_out, g_table, g_w_ada, g_b_ada, g_gain_one, g_wqkv, g_wout, g_gain_two, g_wup, g_bup,
     g_wdown, g_b_down,
-    gathered, table, w_ada, grads, mod_low, table_out, ada_out, wide_out, late_sum, mixed_buf, tok_buf, lines, sem,
+    gathered, w_ada, grads, mod_low, table_out, ada_out, wide_out, late_sum, mixed_buf, tok_buf, lines, sem,
 ):
     pieces = GRAD_ROWS // 192
     targets = [(g_wdown, 0), (g_wup, 768), (g_wout, 1536), (g_wqkv, 1728)]
-    loads = [(gathered_in, gathered), (table_in, table), (w_ada_in, w_ada)]
+    loads = [(gathered_in, gathered), (w_ada_in, w_ada)]
     loads = [pltpu.make_async_copy(src, dst, sem.at[at]) for at, (src, dst) in enumerate(loads)]
     pass_in = [
         pltpu.make_async_copy(mixed_in, mixed_buf, sem.at[3]),
@@ -1099,7 +1114,7 @@
                 wide_out.at[rows], target.at[pl.ds(192 * piece - first, 192)], sem.at[7 + pieces + piece]
             )
         )
-    for copy in grad_in[: pieces // 2] + loads + pass_in + grad_in[pieces // 2 :]:
+    for copy in loads + grad_in + pass_in:
         copy.start()
 
     def widen(piece):
@@ -1108,7 +1123,7 @@
         wide_out[rows, :] = grads[rows, :].astype(f32)
         grad_out[piece].start()
 
-    for piece in range(pieces // 2):
+    for piece in range(pieces // 4):
         widen(piece)
     for copy in loads:
         copy.wait()
@@ -1134,21 +1149,25 @@
     ]
     for copy in line_out:
         copy.start()
-    seqs, steps = early.shape[0], table.shape[0]
-    time_step = early[:, 6, 0:1] * 32.0 + early[:, 7, 0:1]
+    seqs, steps = early.shape[0], table_out.shape[0]
+    time_step = early[:, 6, 0:1] * 32.0 + early[:, 6, 128:129]
     columns = lax.broadcasted_iota(jnp.int32, (seqs, steps), 1).astype(f32)
-    pick = jnp.where(columns == time_step, 1.0, 0.0).astype(f32)
-    picked = lax.dot_general(pick, table[...], NN, precision=highest, preferred_element_type=f32)
-    gate = 1.0 / (1.0 + jnp.exp(-picked))
-    cond = (picked * gate).astype(bf16)
+    pick = jnp.where(columns == time_step, 1.0, 0.0).astype(bf16)
+    cond = early[:, 6, 256:384].astype(bf16)
     ada_out[...] = dot(cond, mod_low[...], TN)
     out_ada = pltpu.make_async_copy(ada_out, g_w_ada, sem.at[7 + 2 * pieces + 5])
     out_ada.start()
-    grad_cond = dot(mod_low[...], w_ada[...], NT) * (gate * (1.0 + picked * (1.0 - gate)))
-    table_out[...] = lax.dot_general(pick, grad_cond, TN, precision=highest, preferred_element_type=f32)
+    grad_cond = dot(mod_low[...], w_ada[...], NT) * (early[:, 6, 384:512] + early[:, 6, 512:640])
+    rest, picked_sum = grad_cond, None
+    for _ in range(3):
+        low = rest.astype(bf16)
+        rest = rest - low.astype(f32)
+        term = dot(pick, low, TN)
+        picked_sum = term if picked_sum is None else picked_sum + term
+    table_out[...] = picked_sum
     out_table = pltpu.make_async_copy(table_out, g_table, sem.at[7 + 2 * pieces + 6])
     out_table.start()
-    for piece in range(pieces // 2, pieces):
+    for piece in range(pieces // 4, pieces):
         widen(piece)
     for at in range(2):
         pass_in[at].wait()
@@ -1168,11 +1187,10 @@
     return pl.pallas_call(
         finish_kernel,
         out_shape=tuple(jax.ShapeDtypeStruct(shape, kind) for shape, kind in shapes),
-        in_specs=[any_space] * 6,
+        in_specs=[any_space] * 5,
         out_specs=[any_space] * len(shapes),
         scratch_shapes=[
             pltpu.VMEM(gathered.shape, bf16),
-            pltpu.VMEM(table.shape, f32),
             pltpu.VMEM(w_ada.shape, bf16),
             pltpu.VMEM(grads.shape, bf16),
             pltpu.VMEM((seqs, 6 * D), bf16),
@@ -1186,7 +1204,7 @@
             pltpu.SemaphoreType.DMA((48,)),
         ],
         compiler_params=pltpu.CompilerParams(vmem_limit_bytes=56 * 1024 * 1024),
-    )(gathered, table, w_ada, grads, mixed, grad_tokens)
+    )(gathered, w_ada, grads, mixed, grad_tokens)
 
 
 def rope_tables():

time: 149 us -> 146 us (0.980)
  Pallas kernels: 148 us -> 145 us
where the time goes in v4:
time: 146 us
  Pallas kernels  145 us (99%)
    pallas_call x1, Pallas kernels, fused_block(): pl.pallas_call(functools.partial(block_kernel, n_bits), out_shape=(jax.Sh...  138 us
    pallas_call x1, Pallas kernels, finish(): pl.pallas_call(finish_kernel, out_shape=tuple((jax.ShapeDtypeStruct(shape...  7.94 us

profile of v4, /device:TPU:0, one launch (start us, length us, event | category | flops | bytes accessed | tf_op | source)
XLA Modules:
  0.0 146.3 jit_solution(14904611884783531325)
XLA Ops:
  0.7 137.5 %shard_map.264 = (bf16[512,768]{1,0:T(8,128)(2,1)}, f32[512,768]{1,0:T(8,128)}, bf16[2,2,16,8,384]{4,3,2,1,0:T(8,128)(2,1)}, bf16[2304,768]{1,0:T(8,128)(2,1)}) custom-call(bf16[512,768]{1,0:T(8,128)(2,1)} %tok_in.1, bf16[512,768]{1,0:T(8,128)(2,1)} %cot_in.1, s32[512]{0:T(512)} %mask_in.1, s32[2]{0:T(128)} %step_in.1, f32[1000,128]{1,0:T(8,128)} %table_in.1, ...), custom_call_target="tpu_custom_call" | custom-call | tf_op jit(solution)/shard_map/pallas_call | solution.py:1071
  138.2 7.9 %shard_map.265 = (bf16[512,768]{1,0:T(8,128)(2,1)}, f32[512,768]{1,0:T(8,128)}, f32[1000,128]{1,0:T(8,128)}, f32[128,4608]{1,0:T(8,128)}, f32[4608]{0:T(1024)}, ...) custom-call(bf16[2,2,16,8,384]{4,3,2,1,0:T(8,128)(2,1)} %get-tuple-e, ...), custom_call_target="tpu_custom_call" | custom-call | tf_op jit(solution)/shard_map/pallas_call | solution.py:1187

commit v5 on v4

--- a/solution.py
+++ b/solution.py
@@ -1114,7 +1114,7 @@
                 wide_out.at[rows], target.at[pl.ds(192 * piece - first, 192)], sem.at[7 + pieces + piece]
             )
         )
-    for copy in loads + grad_in + pass_in:
+    for copy in grad_in[: pieces // 4] + loads + pass_in + grad_in[pieces // 4 :]:
         copy.start()
 
     def widen(piece):
@@ -1127,6 +1127,9 @@
         widen(piece)
     for copy in loads:
         copy.wait()
+    for at in range(2):
+        pass_in[at].wait()
+        pass_out[at].start()
 
     def both(index):
         return jnp.concatenate([gathered[index, 0].astype(f32), gathered[index, 1].astype(f32)], axis=-1)
@@ -1169,9 +1172,6 @@
     out_table.start()
     for piece in range(pieces // 4, pieces):
         widen(piece)
-    for at in range(2):
-        pass_in[at].wait()
-        pass_out[at].start()
     for copy in line_out + [out_ada, out_table] + pass_out + grad_out:
         copy.wait()
 

time: 146 us -> 147 us (level)
  no operation moved by 1% of the time
where the time goes in v5:
time: 147 us
  Pallas kernels  146 us (99%)
    pallas_call x1, Pallas kernels, fused_block(): pl.pallas_call(functools.partial(block_kernel, n_bits), out_shape=(jax.Sh...  138 us
    pallas_call x1, Pallas kernels, finish(): pl.pallas_call(finish_kernel, out_shape=tuple((jax.ShapeDtypeStruct(shape...  8.83 us

profile of v5, /device:TPU:0, one launch (start us, length us, event | category | flops | bytes accessed | tf_op | source)
XLA Modules:
  0.0 147.2 jit_solution(17121192647354658658)
XLA Ops:
  0.7 137.5 %shard_map.264 = (bf16[512,768]{1,0:T(8,128)(2,1)}, f32[512,768]{1,0:T(8,128)}, bf16[2,2,16,8,384]{4,3,2,1,0:T(8,128)(2,1)}, bf16[2304,768]{1,0:T(8,128)(2,1)}) custom-call(bf16[512,768]{1,0:T(8,128)(2,1)} %tok_in.1, bf16[512,768]{1,0:T(8,128)(2,1)} %cot_in.1, s32[512]{0:T(512)} %mask_in.1, s32[2]{0:T(128)} %step_in.1, f32[1000,128]{1,0:T(8,128)} %table_in.1, ...), custom_call_target="tpu_custom_call" | custom-call | tf_op jit(solution)/shard_map/pallas_call | solution.py:1071
  138.2 8.8 %shard_map.265 = (bf16[512,768]{1,0:T(8,128)(2,1)}, f32[512,768]{1,0:T(8,128)}, f32[1000,128]{1,0:T(8,128)}, f32[128,4608]{1,0:T(8,128)}, f32[4608]{0:T(1024)}, ...) custom-call(bf16[2,2,16,8,384]{4,3,2,1,0:T(8,128)(2,1)} %get-tuple-e, ...), custom_call_target="tpu_custom_call" | custom-call | tf_op jit(solution)/shard_map/pallas_call | solution.py:1187
